TPU v7x, 256 devices: a whole 4x4x8 slice. The times are simulated.
256 devices in a mesh: lat: 4 (over x_lo, core), lon: 64 (over x_hi, y, z).
Axes of the slice: x: 4 (x_hi: 2, x_lo: 2; x = x_hi * 2 + x_lo), y: 4, z: 8, core: 2. Of those that a mesh axis runs over, the one named last changes fastest.
Arguments:
- field: bfloat16 [512, 2048, 128], P('lat', 'lon'), may hold values from -6 to 6
- land: int32 [512, 2048], P('lat', 'lon'), may hold values 0 or 1
- mirror: int32 [2048], replicated, may hold values from 0 to 2047, as said below
- depth_weight: bfloat16 [49, 128], replicated, may hold values from -2 to 2
- norm_gain: bfloat16 [128], replicated, may hold values from 0.5 to 2
- up_weight: bfloat16 [128, 512], replicated, may hold values from -0.5 to 0.5
- up_bias: bfloat16 [512], replicated, may hold values from -3 to 3
- down_proj: bfloat16 [512, 128], replicated, may hold values from -0.25 to 0.25
- layer_scale: bfloat16 [128], replicated, may hold values from 0.25 to 1
- section_gain: bfloat16 [3, 128], replicated, may hold values from 0.5 to 2
- section_weight: bfloat16 [3, 512, 128], replicated, may hold values from -0.25 to 0.25
- section_bias: bfloat16 [3, 128], replicated, may hold values from -3 to 3
- cotangent: bfloat16 [64, 256, 128], P('lat', 'lon'), may hold values from -6 to 6
Outputs:
- bottleneck: bfloat16 [64, 256, 128], P('lat', 'lon')
- grad_field: bfloat16 [512, 2048, 128], P('lat', 'lon')
- grad_depth: float32 [49, 128], replicated
- grad_up: float32 [128, 512], replicated
- grad_down: float32 [512, 128], replicated
- grad_section: float32 [3, 512, 128], replicated
Inputs may be any that keep to these rules, and one draw needn't show every extreme that they name: mirror[i] = (s - i) mod 2048 for one s, the same for all i; mirror is its own inverse.
All inputs are finite; a program needn't handle non-finite values. No bound on the sum of `land` on one device may be relied on, other than what follows from the above.
Results may differ from a plain program's by a relative error of at most 0.017.
Values may be sent and summed in bfloat16 or wider, within the bound.
A program may use at most 128 MiB of HBM per device.

v0:
```python
import math

import jax
import jax.numpy as jnp
from jax import lax
from jax.sharding import PartitionSpec as P

SECTIONS = 3


epsilon = 1e-06


def extended_2(array, sides, width, wrap):
    for axis, dim in sides:
        peers, length = (lax.axis_size(axis), array.shape[dim])
        up = [(i, (i + 1) % peers) for i in range(peers if wrap else peers - 1)]
        down = [(j, i) for i, j in up]
        last = lax.slice_in_dim(array, length - width, length, axis=dim)
        leading = lax.slice_in_dim(array, 0, width, axis=dim)
        before = lax.ppermute(last, axis, up)
        after = lax.ppermute(leading, axis, down)
        array = jnp.concatenate([before, array, after], axis=dim)
    return array


def norm_parts(values):
    center = values - jnp.mean(values, axis=-1, keepdims=True)
    rstd = lax.rsqrt(jnp.mean(center * center, axis=-1, keepdims=True) + epsilon)
    return (center * rstd, rstd)


def norm_back(grad_hat, normed_hat, rstd):
    first = jnp.mean(grad_hat, axis=-1, keepdims=True)
    second = jnp.mean(grad_hat * normed_hat, axis=-1, keepdims=True)
    return rstd * (grad_hat - first - normed_hat * second)


def gelu_parts(hidden):
    cdf = 0.5 * (1.0 + jax.scipy.special.erf(hidden * 0.7071067811865476))
    dens = jnp.exp(-0.5 * hidden * hidden) * 0.3989422804014327
    return (hidden * cdf, cdf + hidden * dens)


def extend(values):
    widened = extended_2(values, (("lon", 1),), 3, True)
    return extended_2(widened, (("lat", 0),), 3, False)


def on_device(
    field,
    land,
    mirror,
    depth_weight,
    norm_gain,
    up_weight,
    up_bias,
    down_proj,
    layer_scale,
    section_gain,
    section_weight,
    section_bias,
    cotangent,
):
    row_count, col_count, chan_count = field.shape
    lon_count = lax.axis_size("lon")
    total_cols = col_count * lon_count
    total_rows = row_count * lax.axis_size("lat")
    lon_place = lax.axis_index("lon")
    north = lax.axis_index("lat") == lax.axis_size("lat") - 1
    factor = 1.0 / math.sqrt(total_rows * total_cols / 64.0)
    taps = depth_weight.astype(jnp.float32)
    extended = extend(field)
    top_rows = field[row_count - 3 :][::-1]
    every_top = lax.all_gather(top_rows, "lon", axis=1, tiled=True)
    ext_index = jnp.mod(
        lon_place * col_count - 3 + jnp.arange(col_count + 6, dtype=jnp.int32), total_cols
    )
    folded = jnp.take(every_top, jnp.take(mirror, ext_index), axis=1)
    extended = jnp.concatenate(
        [extended[: row_count + 3], jnp.where(north, folded, extended[row_count + 3 :])], axis=0
    )
    depth_out = jnp.zeros((row_count, col_count, chan_count), jnp.float32)
    for tap in range(49):
        tap_row = tap // 7
        tap_col = tap % 7
        depth_out = (
            depth_out
            + extended[tap_row : tap_row + row_count, tap_col : tap_col + col_count].astype(
                jnp.float32
            )
            * taps[tap]
        )
    depth_hat, depth_rstd = norm_parts(depth_out)
    normed = (depth_hat * norm_gain.astype(jnp.float32)).astype(jnp.bfloat16)
    flat = normed.reshape(-1, chan_count)
    hidden = jnp.dot(flat, up_weight, preferred_element_type=jnp.float32) + up_bias.astype(
        jnp.float32
    )
    active_full, slope = gelu_parts(hidden)
    active = active_full.astype(jnp.bfloat16)
    mixed = jnp.dot(active, down_proj, preferred_element_type=jnp.float32).reshape(
        row_count, col_count, chan_count
    )
    land_f = land.astype(jnp.float32)[:, :, None]
    scale_f = layer_scale.astype(jnp.float32)
    level = (land_f * (field.astype(jnp.float32) + scale_f * mixed)).astype(jnp.bfloat16)
    saved = []
    for section in range(SECTIONS):
        section_hat, section_rstd = norm_parts(level.astype(jnp.float32))
        section_norm = (section_hat * section_gain[section].astype(jnp.float32)).astype(
            jnp.bfloat16
        )
        size_r = section_norm.shape[0]
        size_c = section_norm.shape[1]
        patches = section_norm.reshape(size_r // 2, 2, size_c // 2, 2, chan_count)
        kernel = section_weight[section].reshape(2, 2, chan_count, chan_count)
        level = (
            jnp.einsum("iajbc,abcd->ijd", patches, kernel, preferred_element_type=jnp.float32)
            + section_bias[section].astype(jnp.float32)
        ).astype(jnp.bfloat16)
        saved.append((section_hat, section_rstd, patches, kernel))
    upstream = cotangent
    section_list = [None] * SECTIONS
    for section in range(SECTIONS - 1, -1, -1):
        section_hat, section_rstd, patches, kernel = saved[section]
        section_list[section] = jnp.einsum(
            "iajbc,ijd->abcd", patches, upstream, preferred_element_type=jnp.float32
        ).reshape(4 * chan_count, chan_count)
        spread = jnp.einsum(
            "ijd,abcd->iajbc", upstream, kernel, preferred_element_type=jnp.float32
        ).reshape(section_hat.shape)
        upstream = norm_back(
            spread * section_gain[section].astype(jnp.float32), section_hat, section_rstd
        ).astype(jnp.bfloat16)
    section_total = jnp.stack(section_list)
    direct = land_f * upstream.astype(jnp.float32)
    mix_grad = (direct * scale_f).astype(jnp.bfloat16).reshape(-1, chan_count)
    down_sums = jnp.dot(active.T, mix_grad, preferred_element_type=jnp.float32)
    act_grad = jnp.dot(mix_grad, down_proj.T, preferred_element_type=jnp.float32)
    hidden_grad = (act_grad * slope).astype(jnp.bfloat16)
    up_sums = jnp.dot(flat.T, hidden_grad, preferred_element_type=jnp.float32)
    normed_grad = jnp.dot(hidden_grad, up_weight.T, preferred_element_type=jnp.float32).reshape(
        row_count, col_count, chan_count
    )
    depth_grad = norm_back(
        normed_grad * norm_gain.astype(jnp.float32), depth_hat, depth_rstd
    ).astype(jnp.bfloat16)
    depth_f = depth_grad.astype(jnp.float32)
    tap_list = []
    for tap in range(49):
        tap_row = tap // 7
        tap_col = tap % 7
        tap_list.append(
            jnp.sum(
                extended[tap_row : tap_row + row_count, tap_col : tap_col + col_count].astype(
                    jnp.float32
                )
                * depth_f,
                axis=(0, 1),
            )
        )
    tap_sums = jnp.stack(tap_list)
    spread_back = extend(depth_grad)
    padded = jnp.pad(spread_back, ((3, 3), (3, 3), (0, 0)))
    back_sum = jnp.zeros((row_count + 3, col_count, chan_count), jnp.float32)
    for tap in range(49):
        tap_row = tap // 7
        tap_col = tap % 7
        back_sum = (
            back_sum
            + padded[
                9 - tap_row : 12 - tap_row + row_count, 9 - tap_col : 9 - tap_col + col_count
            ].astype(jnp.float32)
            * taps[tap]
        )
    conv_grad = back_sum[:row_count]
    fold_grad = back_sum[row_count:].astype(jnp.bfloat16)
    own_index = lon_place * col_count + jnp.arange(col_count, dtype=jnp.int32)
    targets = jnp.take(mirror, own_index)
    every_grad = lax.all_gather(fold_grad, "lon", axis=1, tiled=True)
    picked = jnp.take(every_grad, targets, axis=1).astype(jnp.float32)
    lower_rows = conv_grad[row_count - 3 :] + jnp.where(north, picked[::-1], 0.0)
    total_grad = direct + jnp.concatenate([conv_grad[: row_count - 3], lower_rows], axis=0)
    grad_field = total_grad.astype(jnp.bfloat16)
    tap_sums, up_sums, down_sums, section_total = lax.psum(
        (tap_sums, up_sums, down_sums, section_total), ("lat", "lon")
    )
    return (
        level,
        grad_field,
        tap_sums * factor,
        up_sums * factor,
        down_sums * factor,
        section_total * factor,
    )


def solution(mesh):
    in_specs = (
        P("lat", "lon", None),
        P("lat", "lon"),
        P(),
        P(),
        P(),
        P(),
        P(),
        P(),
        P(),
        P(),
        P(),
        P(),
        P("lat", "lon", None),
    )
    out_specs = (P("lat", "lon", None), P("lat", "lon", None), P(), P(), P(), P())
    return jax.shard_map(
        on_device, mesh=mesh, in_specs=in_specs, out_specs=out_specs, check_vma=False
    )
```

profile of v0, /device:TPU:1, one launch (start us, length us, event | category | flops | bytes accessed | tf_op | source)
XLA Modules:
  0.0 649.2 jit_solution(4068497093461746249)
XLA Ops:
  7.3 1.3 fusion.186
  8.6 2.5 collective-permute-start
  11.1 8.9 %collective-permute-start.1 = (bf16[128,3,128]{2,0,1:T(8,128)(2,1)S(1)}, bf16[128,3,128]{2,0,1:T(8,128)(2,1)S(1)}, u32[]{:S(2)}, u32[]{:S(2)}) collective-permute-start(bf16[128,3,128]{2,0,1:T(8,128)(2,1)S(1)} %copy.209), channel_id=1, source_target_pairs={{1,0},{2,1},{3,2},{4,3},{5,4},{6,5},{7,6},{8,7},{9,8},{10,9},{11,1... | collective-permute-start | bytes 294920 | tf_op jit(solution)/shard_map/ppermute | solution.py:22
  21.6 1.5 gather_fusion
  23.6 1.4 gather_fusion.2
  33.3 2.9 collective-permute-start.3
  40.7 2.9 collective-permute-start.2
  43.6 78.9 %all-gather.3.cloned.1.call-done = bf16[3,2048,128]{2,1,0:T(8,128)(2,1)} async-done(((bf16[3,32,128]{2,1,0:T(8,128)(2,1)}), bf16[3,2048,128]{2,1,0:T(8,128)(2,1)}) %all-gather.3.cloned.1.call-update) | async-done | bytes 1572880 | tf_op jit(solution)/shard_map/all_gather | solution.py:75
  122.5 3.2 copy.132
  125.7 1.4 gather_fusion.1
  127.9 22.6 %fusion.182 = (f32[128,32]{0,1:T(8,128)S(1)}, f32[128,32,128]{2,0,1:T(8,128)S(1)}) fusion(f32[128]{0:T(128)} %get-tuple-element.124, bf16[3,38,128]{2,0,1:T(4,128)(2,1)S(1)} %bitcast_select_fusion, bf16[128,38,128]{2,0,1:T(8,128)(2,1)S(1)} %get-tuple-element.122, f32[128]{0:T(128)} %get-tuple-element.125, f32[128]{0:T(128)} %get-tuple-element.126, ...), kind=kLoop, calls=%fused_computation.493 | loop fusion | flops 143126528 | bytes 10782208 | tf_op jit(solution)/shard_map/reduce_sum | solution.py:28
  150.6 1.3 multiply_reduce_fusion.3
  152.0 1.2 multiply_convert_fusion.3
  154.0 4.6 multiply_convert_fusion
  158.6 1.2 fusion.190
  160.6 4.1 convert_reduce_fusion
  164.7 1.3 fusion.16
  166.0 1.5 fusion.11
  173.6 1.5 copy.143
  175.1 1.3 broadcast_multiply_fusion.8
  176.4 1.6 copy.173
  178.0 1.7 reshape.462
  179.7 1.8 multiply_convert_fusion.4
  181.5 2.5 multiply_reduce_fusion.2
  185.3 3.5 fusion.12
  189.4 1.6 copy.148
  191.0 1.4 broadcast_multiply_fusion.3
  192.4 2.1 copy.149
  194.5 2.3 div.71
  196.8 7.5 %multiply_convert_fusion.2 = (bf16[128,32,128]{2,0,1:T(8,128)(2,1)S(1)}, bf16[128,32,128]{2,0,1:T(8,128)(2,1)}) fusion(f32[128]{0:T(128)} %convert_element_type.494, f32[128,32]{0,1:T(8,128)} %convert_element_type.492, f32[128,32]{0,1:T(8,128)} %broadcast_multiply_fusion.12, f32[128,32]{0,1:T(8,128)} %copy-done.36, bf16[128,32,128]{2,0,1:T(8,128)(2,1)} %copy-done.9, ...), kind=kLoop, calls=%fused_computation.273 | loop fusion | flops 6815744 | bytes 5325824 | tf_op jit(solution)/shard_map/convert_element_type | solution.py:138
  205.0 2.0 fusion.192
  207.0 6.9 %fusion.5 = bf16[4096,512]{1,0:T(8,128)(2,1)S(1)} fusion(f32[4096,512]{1,0:T(8,128)} %get-tuple-element.179, bf16[4096,128]{1,0:T(8,128)(2,1)S(1)} %bitcast.315, bf16[512,128]{1,0:T(8,128)(2,1)S(1)} %copy-done.49, f32[512]{0:T(512)S(1)} %copy-done.54), kind=kOutput, calls=%fused_computation.99 | convolution fusion | flops 559939584 | bytes 13764608 | tf_op jit(solution)/shard_map/dot_general | solution.py:140
  213.9 1.5 fusion.191
  215.4 2.6 multiply_reduce_fusion.1
  218.2 3.7 multiply_reduce_fusion
  221.9 7.7 %fusion.113 = (f32[128]{0:T(128)}, f32[128]{0:T(128)}, f32[128]{0:T(128)}, f32[128]{0:T(128)}, f32[128]{0:T(128)}, /*index=5*/f32[128]{0:T(128)}, bf16[128,32,128]{2,0,1:T(8,128)(2,1)S(1)}) fusion(bf16[3,38,128]{2,0,1:T(4,128)(2,1)S(1)} %bitcast_select_fusion, bf16[128,38,128]{2,0,1:T(8,128)(2,1)S(1)} %get-tuple-element.122, ...), kind=kLoop, calls=%fused_computation.262 | loop fusion | flops 23592192 | bytes 6586368 | tf_op jit(solution)/shard_map/reduce_sum | solution.py:155
  229.7 4.1 fusion.114
  233.8 2.0 fusion.94
  236.4 1.6 copy.155
  238.0 1.2 reshape.408
  239.3 1.8 convolution_bitcast_fusion.4
  242.5 1.4 collective-permute-start.4
  243.9 5.8 collective-permute-start.5
  249.8 3.2 fusion.85
  253.0 4.1 fusion.87
  257.3 7.1 %collective-permute-start.6 = (bf16[3,38,128]{2,0,1:T(4,128)(2,1)S(1)}, bf16[3,38,128]{2,0,1:T(4,128)(2,1)S(1)}, u32[]{:S(2)}, u32[]{:S(2)}) collective-permute-start(bf16[3,38,128]{2,0,1:T(4,128)(2,1)S(1)} %get-tuple-element.104), channel_id=1, source_target_pairs={{0,64},{64,128},{128,192},{1,65},{65,129},{129,193},{2,66},{66,130... | collective-permute-start | bytes 87560 | tf_op jit(solution)/shard_map/ppermute | solution.py:21
  264.4 1.9 collective-permute-start.7
  267.4 2.3 collective-permute-done.7
  270.7 1.8 pad_maximum_fusion.1
  272.9 20.2 %multiply_add_fusion = f32[131,32,128]{2,0,1:T(8,128)S(1)} fusion(bf16[131,38,128]{2,0,1:T(8,128)(2,1)S(1)} %get-tuple-element.102, bf16[134,38,128]{2,0,1:T(8,128)(2,1)S(1)} %pad_maximum_fusion, bf16[131,38,128]{2,0,1:T(8,128)(2,1)S(1)} %get-tuple-element.101, f32[128]{0:T(128)S(1)} %copy-done.79, f32[128]{0:T(128)S(1)} %copy-done.80, ...), kind=kLoop, calls=%fused_computation.159 | loop fusion | flops 78340096 | bytes 34689536 | tf_op jit(solution)/shard_map/add | solution.py:171
  293.1 1.4 copy-done.18
  296.5 2.8 fusion.86
  299.3 3.4 fusion.112
  303.0 4.0 fusion.115
  307.5 73.4 %psum.28 = f32[49,128]{1,0:T(8,128)S(1)} all-reduce(f32[49,128]{1,0:T(8,128)S(1)} %stack.202), channel_id=1, replica_groups=mesh['lat'=4,'lon'=64] {'lat','lon'}, use_global_device_ids=true, to_apply=%region_65.66 | all-reduce | flops 6272 | bytes 50176 | tf_op jit(solution)/shard_map/psum | solution.py:186
  381.5 141.3 %all-reduce.4.cloned.1.call-done = (f32[128,512]{1,0:T(8,128)}, f32[512,128]{1,0:T(8,128)}, f32[3,512,128]{2,1,0:T(8,128)}) async-done(((f32[128,512]{1,0:T(8,128)}, f32[512,128]{1,0:T(8,128)}, f32[3,512,128]{2,1,0:T(8,128)}), (f32[128,512]{1,0:T(8,128)}, f32[512,128]{1,0:T(8,128)}, f32[3,512,128]{2,1,0:T(8,128)})) %all-reduce.4.cloned.1.call-update) | async-done | bytes 1310736 | tf_op jit(solution)/shard_map/psum | solution.py:186
  522.8 1.7 broadcast_multiply_fusion.1
  524.5 1.7 broadcast_multiply_fusion.2
  526.1 2.1 broadcast_multiply_fusion
  528.2 103.1 %all-gather.5.cloned.1.call-done = bf16[3,2048,128]{2,1,0:T(8,128)(2,1)} async-done(((bf16[3,32,128]{2,1,0:T(8,128)(2,1)}), bf16[3,2048,128]{2,1,0:T(8,128)(2,1)}) %all-gather.5.cloned.1.call-update) | async-done | bytes 1572880 | tf_op jit(solution)/shard_map/all_gather | solution.py:181
  631.3 4.2 copy.154
  635.5 2.3 gather_fusion.3
  639.0 1.8 fusion.116
  640.8 1.6 copy.162
  (385 shorter events, 33.8 us)
Async XLA Ops:
  7.2 146.8 %copy-start = (bf16[128,512]{1,0:T(8,128)(2,1)S(1)}, bf16[128,512]{1,0:T(8,128)(2,1)}, u32[]{:S(2)}) copy-start(bf16[128,512]{1,0:T(8,128)(2,1)} %param.18) | copy-start | bytes 393220
  7.2 23.2 %copy-start.12 = (bf16[128,32,128]{2,1,0:T(8,128)(2,1)S(1)}, bf16[128,32,128]{2,1,0:T(8,128)(2,1)}, u32[]{:S(2)}) copy-start(bf16[128,32,128]{2,1,0:T(8,128)(2,1)} %param.13) | copy-start | bytes 3145732
  7.2 17.9 %copy-start.58 = (bf16[49,128]{1,0:T(8,128)(2,1)S(1)}, bf16[49,128]{1,0:T(8,128)(2,1)}, u32[]{:S(2)}) copy-start(bf16[49,128]{1,0:T(8,128)(2,1)} %param.16) | copy-start | bytes 37636
  7.2 18.5 %copy-start.106 = (bf16[3,128]{1,0:T(4,128)(2,1)S(1)}, bf16[3,128]{1,0:T(4,128)(2,1)}, u32[]{:S(2)}) copy-start(bf16[3,128]{1,0:T(4,128)(2,1)} %param.22) | copy-start | bytes 2308
  7.2 19.0 %copy-start.107 = (bf16[3,128]{1,0:T(4,128)(2,1)S(1)}, bf16[3,128]{1,0:T(4,128)(2,1)}, u32[]{:S(2)}) copy-start(bf16[3,128]{1,0:T(4,128)(2,1)} %param.24) | copy-start | bytes 2308
  7.2 21.5 %copy-start.38 = (bf16[3,512,128]{2,1,0:T(8,128)(2,1)S(1)}, bf16[3,512,128]{2,1,0:T(8,128)(2,1)}, u32[]{:S(2)}) copy-start(bf16[3,512,128]{2,1,0:T(8,128)(2,1)} %param.23) | copy-start | bytes 1179652
  7.2 22.2 %copy-start.55 = (bf16[16,4,128]{2,1,0:T(4,128)(2,1)S(1)}, bf16[16,4,128]{2,1,0:T(4,128)(2,1)}, u32[]{:S(2)}) copy-start(bf16[16,4,128]{2,1,0:T(4,128)(2,1)} %param.25) | copy-start | bytes 49156
  7.2 115.2 %all-gather.3.cloned.1.call-start = ((), (), s32[]{:S(2)}) async-start(), calls=%async_computation | async-start | bytes 1597440 | tf_op jit(solution)/shard_map/all_gather | solution.py:75
  8.6 21.8 %collective-permute-start = (bf16[128,3,128]{2,0,1:T(8,128)(2,1)S(1)}, bf16[128,3,128]{2,0,1:T(8,128)(2,1)S(1)}, u32[]{:S(2)}, u32[]{:S(2)}) collective-permute-start(bf16[128,3,128]{2,0,1:T(8,128)(2,1)S(1)} %copy.210), channel_id=1, source_target_pairs={{0,1},{1,2},{2,3},{3,4},{4,5},{5,6},{6,7},{7,8},{8,9},{9,10},{10,1... | collective-permute-start | bytes 294920 | tf_op jit(solution)/shard_map/ppermute | solution.py:21
  11.1 20.2 %collective-permute-start.1 = (bf16[128,3,128]{2,0,1:T(8,128)(2,1)S(1)}, bf16[128,3,128]{2,0,1:T(8,128)(2,1)S(1)}, u32[]{:S(2)}, u32[]{:S(2)}) collective-permute-start(bf16[128,3,128]{2,0,1:T(8,128)(2,1)S(1)} %copy.209), channel_id=1, source_target_pairs={{1,0},{2,1},{3,2},{4,3},{5,4},{6,5},{7,6},{8,7},{9,8},{10,9},{11,1... | collective-permute-start | bytes 294920 | tf_op jit(solution)/shard_map/ppermute | solution.py:22
  21.5 501.3 %all-reduce.4.cloned.1.call-start = ((), (), s32[]{:S(2)}) async-start(), calls=%async_computation.2 | async-start | bytes 2621440 | tf_op jit(solution)/shard_map/psum | solution.py:186
  30.4 6.4 copy-start.143
  30.4 6.9 %copy-start.140 = (bf16[512]{0:T(512)(128)(2,1)S(1)}, bf16[512]{0:T(512)(128)(2,1)}, u32[]{:S(2)}) copy-start(bf16[512]{0:T(512)(128)(2,1)} %param.19) | copy-start | bytes 3076
  30.4 7.5 %copy-start.57 = (s32[128,32]{0,1:T(8,128)S(1)}, s32[128,32]{0,1:T(8,128)}, u32[]{:S(2)}) copy-start(s32[128,32]{0,1:T(8,128)} %param.14) | copy-start | bytes 49156
  30.5 8.1 %copy-start.144 = (bf16[128]{0:T(256)(128)(2,1)S(1)}, bf16[128]{0:T(256)(128)(2,1)}, u32[]{:S(2)}) copy-start(bf16[128]{0:T(256)(128)(2,1)} %param.21) | copy-start | bytes 772
  33.3 93.7 %collective-permute-start.3 = (bf16[3,38,128]{2,0,1:T(4,128)(2,1)S(1)}, bf16[3,38,128]{2,0,1:T(4,128)(2,1)}, u32[]{:S(2)}, u32[]{:S(2)}) collective-permute-start(bf16[3,38,128]{2,0,1:T(4,128)(2,1)S(1)} %get-tuple-element.106), channel_id=1, source_target_pairs={{64,0},{128,64},{192,128},{65,1},{129,65},{193,129},{66,2},{130,66... | collective-permute-start | bytes 87560 | tf_op jit(solution)/shard_map/ppermute | solution.py:22
  40.7 87.2 %collective-permute-start.2 = (bf16[3,38,128]{2,0,1:T(4,128)(2,1)}, bf16[3,38,128]{2,0,1:T(4,128)(2,1)S(1)}, u32[]{:S(2)}, u32[]{:S(2)}) collective-permute-start(bf16[3,38,128]{2,0,1:T(4,128)(2,1)} %get-tuple-element.105), channel_id=1, source_target_pairs={{0,64},{64,128},{128,192},{1,65},{65,129},{129,193},{2,66},{66,130... | collective-permute-start | bytes 87560 | tf_op jit(solution)/shard_map/ppermute | solution.py:21
  150.6 67.6 %copy-start.4 = (f32[128,32,128]{2,0,1:T(8,128)}, f32[128,32,128]{2,0,1:T(8,128)S(1)}, u32[]{:S(2)}) copy-start(f32[128,32,128]{2,0,1:T(8,128)S(1)} %get-tuple-element.100) | copy-start | bytes 6291460
  153.9 4.6 copy-start.16
  154.0 4.6 copy-start.48
  160.6 5.5 copy-start.63
  196.8 8.2 %copy-start.3 = (bf16[4096,512]{1,0:T(8,128)(2,1)S(1)}, bf16[4096,512]{1,0:T(8,128)(2,1)}, u32[]{:S(2)}) copy-start(bf16[4096,512]{1,0:T(8,128)(2,1)} %copy-done.2) | copy-start | bytes 12582916
  207.0 6.9 %copy-start.17 = (bf16[128,32,128]{2,1,0:T(8,128)(2,1)S(1)}, bf16[128,32,128]{2,1,0:T(8,128)(2,1)}, u32[]{:S(2)}) copy-start(bf16[128,32,128]{2,1,0:T(8,128)(2,1)} %copy-done.16) | copy-start | bytes 3145732
  239.3 4.6 copy-start.50
  242.5 14.8 %collective-permute-start.4 = (bf16[128,3,128]{2,0,1:T(8,128)(2,1)S(1)}, bf16[128,3,128]{2,0,1:T(8,128)(2,1)S(1)}, u32[]{:S(2)}, u32[]{:S(2)}) collective-permute-start(bf16[128,3,128]{2,0,1:T(8,128)(2,1)S(1)} %copy-done.51), channel_id=1, source_target_pairs={{0,1},{1,2},{2,3},{3,4},{4,5},{5,6},{6,7},{7,8},{8,9},{9,10},{10,1... | collective-permute-start | bytes 294920 | tf_op jit(solution)/shard_map/ppermute | solution.py:21
  243.9 13.1 %copy-start.56 = (bf16[16,4,128]{2,1,0:T(4,128)(2,1)S(1)}, bf16[16,4,128]{2,1,0:T(4,128)(2,1)}, u32[]{:S(2)}) copy-start(bf16[16,4,128]{2,1,0:T(4,128)(2,1)} %param.25) | copy-start | bytes 49156
  243.9 13.4 %collective-permute-start.5 = (bf16[128,3,128]{2,0,1:T(8,128)(2,1)S(1)}, bf16[128,3,128]{2,0,1:T(8,128)(2,1)S(1)}, u32[]{:S(2)}, u32[]{:S(2)}) collective-permute-start(bf16[128,3,128]{2,0,1:T(8,128)(2,1)S(1)} %copy-done.50), channel_id=1, source_target_pairs={{1,0},{2,1},{3,2},{4,3},{5,4},{6,5},{7,6},{8,7},{9,8},{10,9},{11,1... | collective-permute-start | bytes 294920 | tf_op jit(solution)/shard_map/ppermute | solution.py:22
  253.0 13.4 %copy-start.45 = (f32[1,512,128]{2,1,0:T(8,128)S(1)}, f32[1,512,128]{2,1,0:T(8,128)}, u32[]{:S(2)}) copy-start(f32[1,512,128]{2,1,0:T(8,128)} %convolution_bitcast_fusion.3) | copy-start | bytes 786436
  257.3 10.1 %collective-permute-start.6 = (bf16[3,38,128]{2,0,1:T(4,128)(2,1)S(1)}, bf16[3,38,128]{2,0,1:T(4,128)(2,1)S(1)}, u32[]{:S(2)}, u32[]{:S(2)}) collective-permute-start(bf16[3,38,128]{2,0,1:T(4,128)(2,1)S(1)} %get-tuple-element.104), channel_id=1, source_target_pairs={{0,64},{64,128},{128,192},{1,65},{65,129},{129,193},{2,66},{66,130... | collective-permute-start | bytes 87560 | tf_op jit(solution)/shard_map/ppermute | solution.py:21
  264.4 5.3 collective-permute-start.7
  267.4 364.0 %all-gather.5.cloned.1.call-start = ((), (), s32[]{:S(2)}) async-start(), calls=%async_computation.1 | async-start | bytes 1597440 | tf_op jit(solution)/shard_map/all_gather | solution.py:181
  272.9 22.2 %copy-start.27 = (bf16[1,512,128]{2,1,0:T(8,128)(2,1)S(1)}, bf16[1,512,128]{2,1,0:T(8,128)(2,1)}, u32[]{:S(2)}) copy-start(bf16[1,512,128]{2,1,0:T(8,128)(2,1)} %copy-done.26) | copy-start | bytes 393220
  296.5 6.2 copy-start.14
  302.7 4.3 copy-start.108
  302.7 4.3 copy-start.109
  302.7 4.3 copy-start.110
  302.8 4.3 copy-start.111
  302.8 4.3 copy-start.112
  302.8 4.3 copy-start.113
  302.8 4.3 copy-start.114
  302.8 4.3 copy-start.115
  302.8 4.3 copy-start.116
  302.8 4.3 copy-start.117
  302.8 4.3 copy-start.118
  302.8 4.3 copy-start.119
  302.8 4.3 copy-start.122
  302.9 4.3 copy-start.123
  302.9 4.3 copy-start.124
  302.9 4.3 copy-start.125
  302.9 4.3 copy-start.126
  302.9 4.3 copy-start.127
  302.9 4.3 copy-start.128
  302.9 4.3 copy-start.129
  302.9 4.3 copy-start.130
  302.9 4.3 copy-start.131
  302.9 4.3 copy-start.132
  303.0 4.3 copy-start.133
  303.0 4.3 copy-start.134
  303.0 4.3 copy-start.135
  303.0 4.3 copy-start.136
  303.0 4.3 copy-start.137
  528.2 109.6 %copy-start.141 = (pred[32]{0:T(512)(128)(4,1)S(1)}, pred[32]{0:T(512)(128)(4,1)}, u32[]{:S(2)}) copy-start(pred[32]{0:T(512)(128)(4,1)} %compare_and_fusion) | copy-start | bytes 100
  528.2 110.8 %slice-start = ((f32[131,32,128]{2,0,1:T(8,128)}), f32[125,32,128]{2,0,1:T(8,128)S(1)}, s32[]{:S(2)}) async-start(f32[131,32,128]{2,0,1:T(8,128)} %copy-done.18), calls=%async_computation.3 | async-start | bytes 4194304 | tf_op jit(solution)/shard_map/slice | solution.py:184
  528.2 110.8 %copy-start.40 = (f32[128,32]{0,1:T(8,128)S(1)}, f32[128,32]{0,1:T(8,128)}, u32[]{:S(2)}) copy-start(f32[128,32]{0,1:T(8,128)} %convert_element_type.492) | copy-start | bytes 49156
  (93 other events, 221.3 us)
Sparse Core Ops, SparseCore 0:
  21.6 100.8 all-gather.2
  267.5 255.2 all-reduce.3
  526.2 105.0 all-gather.4
where the time goes:
time: 657 us; the launch traced here: 649 us
  waiting for transfers between devices  326 us (50%)
  other arithmetic  125 us (19%)
  blocking collectives  73.4 us (11%)
  local copies, waits for them, and re-layouts  47.5 us (7%)
  starting transfers between devices  33.6 us (5%)
  matrix products  27.4 us (4%)
  between operations  16.4 us (2%)
    psum x1, waiting for transfers between devices, on_device(): lax.psum((tap_sums, up_sums, down_sums, section_total), ('lat', 'lon'))  141 us
    all_gather x1, waiting for transfers between devices, on_device(): every_grad = lax.all_gather(fold_grad, 'lon', axis=1, tiled=True)  103 us
    all_gather x1, waiting for transfers between devices, on_device(): every_top = lax.all_gather(top_rows, 'lon', axis=1, tiled=True)  78.9 us
    psum x1, blocking collectives, on_device(): lax.psum((tap_sums, up_sums, down_sums, section_total), ('lat', 'lon'))  73.4 us
    reduce_sum x8, other arithmetic, on_device(): jnp.sum(extended[tap_row:tap_row + row_count, tap_col:tap_col + col_count...  31.3 us
    reduce_sum x2, other arithmetic, norm_parts(): center = values - jnp.mean(values, axis=-1, keepdims=True)  26.7 us
    add x1, other arithmetic, on_device(): back_sum + padded[9 - tap_row:12 - tap_row + row_count, 9 - tap_col:9 - t...  20.2 us
    ppermute x4, starting transfers between devices, extended_2(): after = lax.ppermute(leading, axis, down)  19.6 us
  transfers between devices with their start and end apart: 11, of which 4 were waited for; matrix products, arithmetic and copies ran while one was open for 11% of the time, Pallas kernels for 0%

commit v1 on v0

v1 whole, which is shorter than its diff:
```python
import functools
import math

import jax
import jax.numpy as jnp
from jax import lax
from jax.experimental import pallas as pl
from jax.experimental.pallas import tpu as pltpu
from jax.sharding import PartitionSpec as P

MESH = pl.DeviceIdType.MESH
F32 = jnp.float32
BF16 = jnp.bfloat16
epsilon = 1e-06

G = 16
RR = 8
CC = 32
C = 128
PITCH = 48
EC = CC + 6
ER = RR + 6
NZ = 8
NH = 8
M = 256
CHUNKS = RR * CC * G // M
POS = M // G


def norm_parts(values):
    center = values - jnp.mean(values, axis=-1, keepdims=True)
    rstd = lax.rsqrt(jnp.mean(center * center, axis=-1, keepdims=True) + epsilon)
    return center * rstd, rstd


def norm_back(grad_hat, normed_hat, rstd):
    first = jnp.mean(grad_hat, axis=-1, keepdims=True)
    second = jnp.mean(grad_hat * normed_hat, axis=-1, keepdims=True)
    return rstd * (grad_hat - first - normed_hat * second)


def gelu_parts(h):
    e = jnp.exp(h * h * -0.5)
    t = 1.0 / (1.0 + jnp.abs(h) * 0.23164189)
    q = ((((0.5307027145 * t - 0.726576013) * t + 0.7107068705) * t - 0.142248368) * t + 0.127414796) * t
    q = q * e
    cdf = jnp.where(h >= 0.0, 1.0 - q, q)
    return h * cdf, cdf + h * (e * 0.3989422804014327)


def dot(a, b, ca, cb):
    return lax.dot_general(a, b, (((ca,), (cb,)), ((), ())), preferred_element_type=F32)


def rows(start, size, align=16):
    return pl.ds(pl.multiple_of(start, align), size)


def kernel(
    factor,
    mirror,
    field,
    land,
    taps_in,
    gain_in,
    up,
    bias_in,
    down,
    scale_in,
    sgain_in,
    sw,
    sbias_in,
    cot,
    bott,
    gfield,
    gtaps,
    gup,
    gdown,
    gsec,
    fbuf,
    ext,
    ext2,
    obuf,
    sh,
    wb,
    hat,
    rstd,
    normed,
    act,
    slope,
    landb,
    lev0,
    lev1,
    lev2,
    hat1,
    rstd1,
    hat2,
    rstd2,
    hat3,
    rstd3,
    p1,
    p2,
    p3,
    back1,
    back2,
    direct,
    dgb,
    upacc,
    dtacc,
    secacc,
    tapacc,
    a32,
    s1,
    r1,
    s2f,
    s2,
    r2,
    s3,
    r3,
    r4,
    g3,
    g2,
    g1a,
    g1b,
    tl,
    th,
    tz,
    stl,
    str_,
    cl,
    cr,
    rs,
    rn,
    csl,
    csr,
    cnl,
    cnr,
    dcl,
    dcr,
    rst,
    rsb,
    drs,
    drn,
    dsl,
    dsr,
    dnl,
    dnr,
    fr1,
    fs2,
    fr2,
    fcat,
    zbuf,
    fg,
    hr1,
    hs2,
    hr2,
    ssem,
    rsem,
):
    lat = lax.axis_index("lat")
    lon = lax.axis_index("lon")
    hi, z = lon // NZ, lax.rem(lon, NZ)
    core, xl = lax.rem(lat, 2), lat // 2
    right, left = lax.rem(lon + 1, NH * NZ), lax.rem(lon + NH * NZ - 1, NH * NZ)
    north, south = lat == 3, lat == 0

    counter = [0]

    def take(n):
        counter[0] += n
        return counter[0] - n

    def remote(src, dst, sem, to):
        return pltpu.make_async_remote_copy(
            src_ref=src,
            dst_ref=dst,
            send_sem=ssem.at[sem],
            recv_sem=rsem.at[sem],
            device_id=to,
            device_id_type=MESH,
        )

    def hi_peer(j):
        h = lax.rem(hi + j, NH)
        return h, (lat, h * NZ + z)

    def z_peer(j):
        t = lax.rem(z + j, NZ)
        return t, (lat, hi * NZ + t)

    barrier = pltpu.get_barrier_semaphore()

    def greet(to):
        pl.semaphore_signal(barrier, inc=1, device_id=to, device_id_type=MESH)

    greet((lat, left))
    greet((lat, right))
    for dl in (-1, 1):

        @pl.when((lat + dl >= 0) & (lat + dl < 4))
        def _():
            greet((lat + dl, left))
            greet((lat + dl, right))

    for j in range(1, 4):
        greet((lax.rem(lat + j, 4), lon))
    for j in range(1, NH):
        greet(hi_peer(j)[1])
    for j in range(1, NZ):
        greet(z_peer(j)[1])

    @pl.loop(0, 128)
    def _(i):
        fbuf[rows((i + 3) * PITCH + 8, CC, 8), :] = field[i].astype(F32)

    for j in range(3):
        stl[j] = fbuf[pl.ds(3 * PITCH + 8 + j, 128, stride=PITCH), :].astype(BF16)
        str_[j] = fbuf[pl.ds(3 * PITCH + 8 + CC - 3 + j, 128, stride=PITCH), :].astype(BF16)

    waits = 2 + 3 + (NH - 1) + (NZ - 1)
    pl.semaphore_wait(barrier, waits + jnp.where(south | north, 2, 4))

    def halo_copies(pieces):
        made = []
        for dl, dn, src, dst in pieces:
            sem = take(1)
            to_lon = right if dn == 1 else left if dn == -1 else lon
            copy = remote(src, dst, sem, (lat + dl, to_lon))
            made.append((dl, copy))
        return made

    def when_lat(dl, ok, fn):
        if dl == 0:
            fn()
        else:
            pl.when(ok)(fn)

    def halo_start(made):
        for dl, copy in made:
            when_lat(dl, (lat + dl >= 0) & (lat + dl < 4), copy.start)

    def halo_wait(made):
        for dl, copy in made:
            when_lat(dl, (lat + dl >= 0) & (lat + dl < 4), copy.wait_send)
            when_lat(dl, (lat - dl >= 0) & (lat - dl < 4), copy.wait_recv)

    halo = halo_copies(
        [
            (0, -1, stl, cr),
            (0, 1, str_, cl),
            (1, 0, field.at[pl.ds(125, 3)], rs),
            (-1, 0, field.at[pl.ds(0, 3)], rn),
            (1, 1, str_.at[:, pl.ds(112, 16)], csl),
            (1, -1, stl.at[:, pl.ds(112, 16)], csr),
            (-1, 1, str_.at[:, pl.ds(0, 16)], cnl),
            (-1, -1, stl.at[:, pl.ds(0, 16)], cnr),
        ]
    )
    halo_start(halo)

    shift = mirror[0]
    total = NH * NZ * CC

    def first_block(dev, width):
        base = lax.rem(shift - CC * dev - (width - 1) + (3 if width > CC else 0) + 2 * total, total)
        return base // CC, lax.rem(base, CC)

    def fold_exchange(src, buf1, stage2, buf2, width):
        sem1, sem2 = take(NH - 1), take(NZ - 1)

        def first():
            for j in range(1, NH):
                remote(src, buf1.at[hi], sem1 + j - 1, hi_peer(j)[1]).start()
            buf1[hi] = src[...]

        def held(dev):
            q = first_block(dev, width)[0]
            block = lax.rem(q + lax.rem(z + NH * NZ - q, NZ), NH * NZ)
            return block // NZ

        def second():
            for j in range(1, NH):
                h = lax.rem(hi + NH - j, NH)
                copy = remote(src, buf1.at[h], sem1 + j - 1, hi_peer(j)[1])
                copy.wait_send()
                copy.wait_recv()
            for j in range(1, NZ):
                t, to = z_peer(j)
                stage2[j - 1] = buf1[held(hi * NZ + t)]
                remote(stage2.at[j - 1], buf2.at[z], sem2 + j - 1, to).start()
            buf2[z] = buf1[held(lon)]

        def last():
            for j in range(1, NZ):
                t = lax.rem(z + NZ - j, NZ)
                copy = remote(stage2.at[j - 1], buf2.at[t], sem2 + j - 1, z_peer(j)[1])
                copy.wait_send()
                copy.wait_recv()
            q, off = first_block(lon, width)
            for m in range(3 if width > CC else 2):
                fcat[:, pl.ds(m * CC, CC), :] = buf2[lax.rem(q + m, NZ)].astype(F32)
            return off

        return first, second, last

    fold1, fold2, fold3 = fold_exchange(field.at[pl.ds(125, 3)], fr1, fs2, fr2, CC + 6)
    pl.when(north)(fold1)

    tapf = taps_in[...].astype(F32)
    for t in range(49):
        wb[t] = jnp.broadcast_to(tapf[t : t + 1], (G, C))
    gain = gain_in[...].astype(F32)
    bias = bias_in[...].astype(F32)
    scale = scale_in[...].astype(F32)

    @pl.loop(0, CHUNKS)
    def _(k):
        turned = pltpu.roll(land[...], lax.rem(256 - k * POS, 256), 1)
        for j in range(POS):
            landb[rows((k * POS + j) * G, G), :] = jnp.broadcast_to(turned[:, j : j + 1], (G, C))

    def gather_rows(r0, r1, c0, c1):
        @pl.loop(r0, r1)
        def _(r):
            for c in range(c0, c1):
                ext[rows((r * EC + c) * G, G), :] = fbuf[
                    pl.ds(r * PITCH + 5 + c, G, stride=RR * PITCH), :
                ]

    halo_wait(halo)
    for j in range(3):
        fbuf[pl.ds(3 * PITCH + 5 + j, 128, stride=PITCH), :] = cl[j].astype(F32)
        fbuf[pl.ds(3 * PITCH + 8 + CC + j, 128, stride=PITCH), :] = cr[j].astype(F32)

    @pl.when(south)
    def _():
        fbuf[pl.ds(0, 3 * PITCH), :] = jnp.zeros((3 * PITCH, C), F32)

    @pl.when(jnp.logical_not(south))
    def _():
        for k in range(3):
            fbuf[pl.ds(k * PITCH + 8, CC), :] = rs[k].astype(F32)
            for j in range(3):
                fbuf[pl.ds(k * PITCH + 5 + j, 1), :] = csl[j].astype(F32)[13 + k : 14 + k]
                fbuf[pl.ds(k * PITCH + 8 + CC + j, 1), :] = csr[j].astype(F32)[13 + k : 14 + k]

    @pl.when(jnp.logical_not(north))
    def _():
        for k in range(3):
            fbuf[pl.ds((131 + k) * PITCH + 8, CC), :] = rn[k].astype(F32)
            for j in range(3):
                fbuf[pl.ds((131 + k) * PITCH + 5 + j, 1), :] = cnl[j].astype(F32)[k : k + 1]
                fbuf[pl.ds((131 + k) * PITCH + 8 + CC + j, 1), :] = cnr[j].astype(F32)[k : k + 1]

    gather_rows(0, 11, 0, EC)
    pl.when(north)(fold2)

    def conv(src, r, cb, flip):
        total_ = None
        for a in range(7):
            for b in range(7):
                t = 48 - (7 * a + b) if flip else 7 * a + b
                x = src[rows(((r + a) * EC + cb * 8 + b) * G, 8 * G), :].reshape(8, G, C)
                term = x * wb[t][None]
                total_ = term if total_ is None else total_ + term
        return total_

    def depth_rows(r0, r1):
        @pl.loop(r0, r1)
        def _(r):
            @pl.loop(0, 4)
            def _(cb):
                h, s = norm_parts(conv(ext, r, cb, False).reshape(8 * G, C))
                at = rows((r * CC + cb * 8) * G, 8 * G)
                hat[at, :] = h
                rstd[at, :] = jnp.broadcast_to(s, h.shape)
                normed[at, :] = (h * gain).astype(BF16)

    depth_rows(0, 5)

    @pl.when(north)
    def _():
        off = fold3()
        for k in range(3):
            for i in range(EC):
                fbuf[pl.ds((131 + k) * PITCH + 5 + i, 1), :] = fcat[2 - k, pl.ds(off + EC - 1 - i, 1), :]

    gather_rows(11, 14, 0, EC)
    depth_rows(5, 8)

    @pl.loop(0, CHUNKS)
    def _(k):
        at = rows(k * M, M)
        r, c0 = k // 2, lax.rem(k, 2) * POS
        h = dot(normed[at, :], up[...], 1, 0) + bias
        active, slp = gelu_parts(h)
        active = active.astype(BF16)
        act[at, :] = active
        slope[at, :] = slp.astype(BF16)
        mixed = dot(active, down[...], 1, 0)
        x = ext[rows(((r + 3) * EC + 3 + c0) * G, M), :]
        lev0[at, :] = (landb[at, :] * (x + scale * mixed)).astype(BF16)

    def section(s, count, cols, src, hats, rstds, patches, put):
        sg = sgain_in[s : s + 1].astype(F32)
        sb = sbias_in[s : s + 1].astype(F32)
        n = cols * G
        half = cols // 2

        def step(i):
            parts = []
            for a in range(2):
                at = rows((2 * i + a) * n, n)
                h, rs_ = norm_parts(src[at, :].astype(F32))
                hats[at, :] = h
                rstds[at, :] = jnp.broadcast_to(rs_, h.shape)
                sn = (h * sg).astype(BF16).reshape(half, 2, G, C)
                parts += [sn[:, b].reshape(half * G, C) for b in range(2)]
            p = jnp.concatenate(parts, axis=1)
            patches[rows(i * half * G, half * G), :] = p
            put(i, (dot(p, sw[s], 1, 0) + sb).astype(BF16))

        if count == 1:
            step(0)
        else:
            pl.loop(0, count)(step)

    def put1(i, v):
        lev1[rows(i * 256, 256), :] = v

    def put2(i, v):
        lev2[rows(i * 128, 128), :] = v

    def put3(i, v):
        bott[...] = v

    section(0, 4, 32, lev0, hat1, rstd1, p1, put1)
    section(1, 2, 16, lev1, hat2, rstd2, p2, put2)
    section(2, 1, 8, lev2, hat3, rstd3, p3, put3)

    def section_back(s, count, cols, src, hats, rstds, patches, put):
        sg = sgain_in[s : s + 1].astype(F32)
        n = cols * G
        half = cols // 2
        secacc[s] = jnp.zeros((4 * C, C), F32)

        def step(i):
            at = rows(i * half * G, half * G)
            u = src[at, :]
            secacc[s] += dot(patches[at, :], u, 0, 0)
            spread = dot(u, sw[s], 1, 1)
            for a in range(2):
                at2 = rows((2 * i + a) * n, n)
                hh = hats[at2, :].reshape(half, 2, G, C)
                rr = rstds[at2, :].reshape(half, 2, G, C)
                outs = []
                for b in range(2):
                    q = 2 * a + b
                    g = (spread[:, q * C : (q + 1) * C] * sg).reshape(half, G, C)
                    outs.append(norm_back(g, hh[:, b], rr[:, b]).astype(BF16))
                put(at2, jnp.stack(outs, axis=1).reshape(n, C))

        if count == 1:
            step(0)
        else:
            pl.loop(0, count)(step)

    def putb2(at, v):
        back2[at, :] = v

    def putb1(at, v):
        back1[at, :] = v

    def putb0(at, v):
        direct[at, :] = (landb[at, :] * v.astype(F32)).astype(BF16)

    section_back(2, 1, 8, cot, hat3, rstd3, p3, putb2)
    section_back(1, 2, 16, back2, hat2, rstd2, p2, putb1)
    section_back(0, 4, 32, back1, hat1, rstd1, p1, putb0)

    upacc[...] = jnp.zeros_like(upacc)
    dtacc[...] = jnp.zeros_like(dtacc)

    @pl.loop(0, CHUNKS)
    def _(k):
        at = rows(k * M, M)
        r, c0 = k // 2, lax.rem(k, 2) * POS
        mg = (direct[at, :].astype(F32) * scale).astype(BF16)
        dtacc[...] += dot(mg, act[at, :], 0, 0)
        hg = (dot(mg, down[...], 1, 1) * slope[at, :].astype(F32)).astype(BF16)
        upacc[...] += dot(normed[at, :], hg, 0, 0)
        ng = dot(hg, up[...], 1, 1) * gain
        dg = norm_back(ng, hat[at, :], rstd[at, :]).astype(BF16)
        dgb[r, pl.ds(c0, POS)] = dg.reshape(POS, G, C)
        ext2[rows(((r + 3) * EC + 3 + c0) * G, M), :] = dg.astype(F32)

    for i in range(3):
        rst[i] = ext2[pl.ds(((8 + i) * EC + 3) * G + 15, CC, stride=G), :].astype(BF16)
        rsb[i] = ext2[pl.ds(((3 + i) * EC + 3) * G, CC, stride=G), :].astype(BF16)

    halo2 = halo_copies(
        [
            (0, -1, dgb.at[:, pl.ds(0, 3)], dcr),
            (0, 1, dgb.at[:, pl.ds(CC - 3, 3)], dcl),
            (1, 0, rst, drs),
            (-1, 0, rsb, drn),
            (1, 1, rst.at[:, pl.ds(16, 16)], dsl),
            (1, -1, rst.at[:, pl.ds(0, 16)], dsr),
            (-1, 1, rsb.at[:, pl.ds(16, 16)], dnl),
            (-1, -1, rsb.at[:, pl.ds(0, 16)], dnr),
        ]
    )
    halo_start(halo2)

    for q in range(4):
        a32[pl.ds(q * C, C), :] = upacc[:, q * C : (q + 1) * C]
        a32[pl.ds((4 + q) * C, C), :] = dtacc[:, q * C : (q + 1) * C].T
    for s in range(3):
        a32[pl.ds((8 + 4 * s) * C, 4 * C), :] = secacc[s]
    s1[...] = a32[...].astype(BF16)

    core_to, x_to = (lat + 1 - 2 * core, lon), (lax.rem(lat + 2, 4), lon)
    c1 = remote(s1.at[rows((1 - core) * 1280, 1280)], r1, take(1), core_to)
    c1.start()

    def sum_taps(r0, r1_):
        @pl.loop(r0, r1_)
        def _(r):
            @pl.loop(0, 4)
            def _(cb):
                d = ext2[rows(((r + 3) * EC + 3 + cb * 8) * G, 8 * G), :]
                for a in range(7):
                    for b in range(7):
                        x = ext[rows(((r + a) * EC + cb * 8 + b) * G, 8 * G), :]
                        tapacc[7 * a + b] += jnp.sum((x * d).reshape(16, 8, C), axis=0)

    tapacc[...] = jnp.zeros_like(tapacc)
    sum_taps(0, 2)

    c1.wait()
    s2f[...] = a32[rows(core * 1280, 1280), :] + r1[...].astype(F32)
    s2[...] = s2f[...].astype(BF16)
    c2 = remote(s2.at[rows((1 - xl) * 640, 640)], r2, take(1), x_to)
    c2.start()
    sum_taps(2, 4)
    c2.wait()
    s3[...] = (s2f[rows(xl * 640, 640), :] + r2[...].astype(F32)).astype(BF16)
    sem3 = take(NH - 1)
    for j in range(1, NH):
        h, to = hi_peer(j)
        remote(s3.at[rows(h * 80, 80)], r3.at[hi], sem3 + j - 1, to).start()
    r3[hi] = s3[rows(hi * 80, 80), :]
    sum_taps(4, 8)

    def tap_stage(buf, peers, me):
        sem = take(len(peers))

        def start(value):
            buf[me] = value
            for i, (_, to) in enumerate(peers):
                remote(buf.at[me], buf.at[me], sem + i, to).start()

        def finish():
            for i, (frm, to) in enumerate(peers):
                copy = remote(buf.at[me], buf.at[frm], sem + i, to)
                copy.wait_send()
                copy.wait_recv()
            out = buf[0]
            for i in range(1, buf.shape[0]):
                out = out + buf[i]
            return out

        return start, finish

    lat_peers = [(lax.rem(lat + 4 - j, 4), (lax.rem(lat + j, 4), lon)) for j in range(1, 4)]
    hi_peers = [(lax.rem(hi + NH - j, NH), hi_peer(j)[1]) for j in range(1, NH)]
    z_peers = [(lax.rem(z + NZ - j, NZ), z_peer(j)[1]) for j in range(1, NZ)]
    tl_start, tl_finish = tap_stage(tl, lat_peers, lat)
    th_start, th_finish = tap_stage(th, hi_peers, hi)
    tz_start, tz_finish = tap_stage(tz, z_peers, z)
    tl_start(jnp.concatenate([jnp.sum(tapacc[...], axis=1), jnp.zeros((15, C), F32)], axis=0))

    halo_wait(halo2)

    @pl.when(south)
    def _():
        drs[...] = jnp.zeros_like(drs)
        dsl[...] = jnp.zeros_like(dsl)
        dsr[...] = jnp.zeros_like(dsr)

    @pl.when(north)
    def _():
        drn[...] = jnp.zeros_like(drn)
        dnl[...] = jnp.zeros_like(dnl)
        dnr[...] = jnp.zeros_like(dnr)

    @pl.loop(0, RR)
    def _(r):
        for j in range(3):
            ext2[rows(((r + 3) * EC + j) * G, G), :] = dcl[r, j].astype(F32)
            ext2[rows(((r + 3) * EC + 3 + CC + j) * G, G), :] = dcr[r, j].astype(F32)

    fg1, fg2, fg3 = fold_exchange(fg, hr1, hs2, hr2, CC)

    @pl.when(north)
    def _():
        for i in range(3):
            for cut, at in ((0, 0), (8, 8), (16, 16), (24, 24), (30, 30)):
                zbuf[i, pl.ds(at, 8), :] = ext2[pl.ds(((8 + i) * EC + cut) * G + 15, 8, stride=G), :]
        for k in range(1, 4):
            total_ = None
            for a in range(k + 3, 7):
                for b in range(7):
                    term = zbuf[k - a + 5, pl.ds(6 - b, CC), :] * wb[7 * a + b][0:1]
                    total_ = term if total_ is None else total_ + term
            fg[k - 1] = total_.astype(BF16)
        fg1()

    for k in range(6):
        low = k < 3
        r = k + 5 if low else k - 3
        edge, el, er = (drs, dsl, dsr) if low else (drn, dnl, dnr)
        i = k if low else k - 3
        line = 7 if low else 24
        for c in range(EC):
            sh[pl.ds(c * 32 + 8, G), :] = ext2[pl.ds(((r + 3) * EC + c) * G, G), :]
        sh[pl.ds(3 * 32 + line, CC, stride=32), :] = edge[i].astype(F32)
        lft, rgt = el[i].astype(F32), er[i].astype(F32)
        for j in range(3):
            sh[pl.ds(j * 32 + line, 1), :] = lft[13 + j : 14 + j]
            sh[pl.ds((CC + 3 + j) * 32 + line, 1), :] = rgt[j : j + 1]
        to = k if low else k + 8
        for c in range(EC):
            ext2[pl.ds((to * EC + c) * G, G), :] = sh[pl.ds(c * 32 + (7 if low else 9), G), :]

    def grad_rows(r0, r1_):
        @pl.loop(r0, r1_)
        def _(r):
            @pl.loop(0, 4)
            def _(cb):
                v = conv(ext2, r, cb, True)
                v = v + direct[rows((r * CC + cb * 8) * G, 8 * G), :].astype(F32).reshape(8, G, C)
                for j in range(8):
                    obuf[pl.ds(r * CC + cb * 8 + j, G, stride=RR * CC), :] = v[j]

    for j in range(1, NH):
        h = lax.rem(hi + NH - j, NH)
        copy = remote(s3.at[pl.ds(0, 80)], r3.at[h], sem3 + j - 1, hi_peer(j)[1])
        copy.wait_send()
        copy.wait_recv()
    part = r3[0].astype(F32)
    for i in range(1, NH):
        part = part + r3[i].astype(F32)
    r4[z] = part.astype(BF16)
    sem4 = take(NZ - 1)
    for j in range(1, NZ):
        remote(r4.at[z], r4.at[z], sem4 + j - 1, z_peer(j)[1]).start()
    grad_rows(0, 2)

    th_start(tl_finish())
    pl.when(north)(fg2)
    for j in range(1, NZ):
        t = lax.rem(z + NZ - j, NZ)
        copy = remote(r4.at[z], r4.at[t], sem4 + j - 1, z_peer(j)[1])
        copy.wait_send()
        copy.wait_recv()
    part = r4[0].astype(F32)
    for i in range(1, NZ):
        part = part + r4[i].astype(F32)
    g3[hi] = part.astype(BF16)
    sem5 = take(NH - 1)
    for j in range(1, NH):
        remote(g3.at[hi], g3.at[hi], sem5 + j - 1, hi_peer(j)[1]).start()
    grad_rows(2, 4)

    tz_start(th_finish())
    for j in range(1, NH):
        h = lax.rem(hi + NH - j, NH)
        copy = remote(g3.at[hi], g3.at[h], sem5 + j - 1, hi_peer(j)[1])
        copy.wait_send()
        copy.wait_recv()
    x6 = remote(g3, g2, take(1), x_to)
    x7 = remote(g3, g1a, take(1), core_to)
    x8 = remote(g2, g1b, take(1), core_to)
    x6.start()
    x7.start()
    grad_rows(4, 6)
    x6.wait_recv()
    x8.start()
    gtaps[...] = tz_finish()[:49] * factor
    grad_rows(6, 8)

    @pl.when(north)
    def _():
        off = fg3()
        for k in range(1, 4):
            for i in range(CC):
                at = pl.ds((128 - k) * CC + i, 1)
                obuf[at, :] += fcat[k - 1, pl.ds(off + CC - 1 - i, 1), :]

    @pl.loop(0, 128)
    def _(i):
        gfield[i] = obuf[rows(i * CC, CC), :].astype(BF16)

    x6.wait_send()
    x7.wait()
    x8.wait()

    def place(c_, x_, v):
        a32[rows((c_ * 2 + x_) * 640, 640), :] = v.reshape(640, C).astype(F32) * factor

    place(core, xl, g3[...])
    place(core, 1 - xl, g2[...])
    place(1 - core, xl, g1a[...])
    place(1 - core, 1 - xl, g1b[...])
    for q in range(4):
        gup[:, q * C : (q + 1) * C] = a32[pl.ds(q * C, C), :]
        gdown[pl.ds(q * C, C), :] = a32[pl.ds((4 + q) * C, C), :]
    for s in range(3):
        gsec[s] = a32[pl.ds((8 + 4 * s) * C, 4 * C), :]


def on_device(field, land, mirror, depth_weight, norm_gain, up_weight, up_bias, down_proj, layer_scale, section_gain, section_weight, section_bias, cotangent):
    factor = 1.0 / math.sqrt(512 * 2048 / 64.0)
    land_t = land.astype(F32).reshape(G, RR * CC)
    cot_t = jnp.transpose(cotangent, (1, 0, 2)).reshape(4 * G, C)
    vm = pl.BlockSpec(memory_space=pltpu.VMEM)
    n = RR * CC * G

    def f(*shape):
        return pltpu.VMEM(shape, F32)

    def h(*shape):
        return pltpu.VMEM(shape, BF16)

    sems = 96
    scratch = dict(
        fbuf=f(134 * PITCH, C),
        ext=f(ER * EC * G, C),
        ext2=f(ER * EC * G, C),
        obuf=f(n, C),
        sh=f(EC * 32, C),
        wb=f(49, G, C),
        hat=f(n, C),
        rstd=f(n, C),
        normed=h(n, C),
        act=h(n, 512),
        slope=h(n, 512),
        landb=f(n, C),
        lev0=h(n, C),
        lev1=h(n // 4, C),
        lev2=h(n // 16, C),
        hat1=f(n, C),
        rstd1=f(n, C),
        hat2=f(n // 4, C),
        rstd2=f(n // 4, C),
        hat3=f(n // 16, C),
        rstd3=f(n // 16, C),
        p1=h(n // 4, 512),
        p2=h(n // 16, 512),
        p3=h(n // 64, 512),
        back1=h(n // 4, C),
        back2=h(n // 16, C),
        direct=h(n, C),
        dgb=h(RR, CC, G, C),
        upacc=f(C, 512),
        dtacc=f(C, 512),
        secacc=f(3, 512, C),
        tapacc=f(49, 8, C),
        a32=f(2560, C),
        s1=h(2560, C),
        r1=h(1280, C),
        s2f=f(1280, C),
        s2=h(1280, C),
        r2=h(640, C),
        s3=h(640, C),
        r3=h(NH, 80, C),
        r4=h(NZ, 80, C),
        g3=h(NH, 80, C),
        g2=h(NH, 80, C),
        g1a=h(NH, 80, C),
        g1b=h(NH, 80, C),
        tl=f(4, 64, C),
        th=f(NH, 64, C),
        tz=f(NZ, 64, C),
        stl=h(3, 128, C),
        str_=h(3, 128, C),
        cl=h(3, 128, C),
        cr=h(3, 128, C),
        rs=h(3, CC, C),
        rn=h(3, CC, C),
        csl=h(3, 16, C),
        csr=h(3, 16, C),
        cnl=h(3, 16, C),
        cnr=h(3, 16, C),
        dcl=h(RR, 3, G, C),
        dcr=h(RR, 3, G, C),
        rst=h(3, CC, C),
        rsb=h(3, CC, C),
        drs=h(3, CC, C),
        drn=h(3, CC, C),
        dsl=h(3, 16, C),
        dsr=h(3, 16, C),
        dnl=h(3, 16, C),
        dnr=h(3, 16, C),
        fr1=h(NH, 3, CC, C),
        fs2=h(NZ - 1, 3, CC, C),
        fr2=h(NZ, 3, CC, C),
        fcat=f(3, 3 * CC, C),
        zbuf=f(3, 40, C),
        fg=h(3, CC, C),
        hr1=h(NH, 3, CC, C),
        hs2=h(NZ - 1, 3, CC, C),
        hr2=h(NZ, 3, CC, C),
        ssem=pltpu.SemaphoreType.DMA((sems,)),
        rsem=pltpu.SemaphoreType.DMA((sems,)),
    )
    bott, gfield, gtaps, gup, gdown, gsec = pl.pallas_call(
        functools.partial(kernel, factor),
        out_shape=(
            jax.ShapeDtypeStruct((4 * G, C), BF16),
            jax.ShapeDtypeStruct((128, CC, C), BF16),
            jax.ShapeDtypeStruct((49, C), F32),
            jax.ShapeDtypeStruct((C, 512), F32),
            jax.ShapeDtypeStruct((512, C), F32),
            jax.ShapeDtypeStruct((3, 512, C), F32),
        ),
        in_specs=[pl.BlockSpec(memory_space=pltpu.SMEM)] + [vm] * 12,
        out_specs=(vm,) * 6,
        scratch_shapes=list(scratch.values()),
        compiler_params=pltpu.CompilerParams(
            collective_id=0, has_side_effects=True, vmem_limit_bytes=67043328
        ),
    )(
        mirror,
        field,
        land_t,
        depth_weight,
        norm_gain.reshape(1, C),
        up_weight,
        up_bias.reshape(1, 512),
        down_proj,
        layer_scale.reshape(1, C),
        section_gain,
        section_weight,
        section_bias,
        cot_t,
    )
    bott = jnp.transpose(bott.reshape(4, G, C), (1, 0, 2))
    return bott, gfield, gtaps, gup, gdown, gsec


def solution(mesh):
    cell = P("lat", "lon", None)
    in_specs = (cell, P("lat", "lon")) + (P(),) * 10 + (cell,)
    out_specs = (cell, cell, P(), P(), P(), P())
    return jax.shard_map(
        on_device, mesh=mesh, in_specs=in_specs, out_specs=out_specs, check_vma=False
    )
```

time: 657 us -> 108 us (0.16); the launches traced: 649 us -> 107 us
  waiting for transfers between devices: 326 us -> 0 us
  other arithmetic: 125 us -> 0.73 us
  Pallas kernels: 0 us -> 96.7 us
  blocking collectives: 73.4 us -> 0 us
  local copies, waits for them, and re-layouts: 47.5 us -> 9.21 us
  starting transfers between devices: 33.6 us -> 0 us
  matrix products: 27.4 us -> 0 us
  between operations: 16.4 us -> 0.66 us
    all_gather x2 -> x0, waiting for transfers between devices: 182 us -> none  [the longest x1 103 us: on_device(): every_grad = lax.all_gather(fold_grad, 'lon', axis=1, tiled=True)]
    psum x1 -> x0, waiting for transfers between devices: 141 us -> none  [on_device(): lax.psum((tap_sums, up_sums, down_sums, section_total), ('lat', 'lon'))]
    pallas_call x0 -> x1, Pallas kernels: none -> 96.7 us  [on_device(): pl.pallas_call(functools.partial(kernel, factor), out_shape=(jax.ShapeDty...]
    psum x1 -> x0, blocking collectives: 73.4 us -> none  [on_device(): lax.psum((tap_sums, up_sums, down_sums, section_total), ('lat', 'lon'))]
    reduce_sum x18 -> x0, other arithmetic: 68.9 us -> none  [the longest x8 31.3 us: on_device(): jnp.sum(extended[tap_row:tap_row + row_count, tap_col:tap_col + col_count...]
    ppermute x8 -> x0, starting transfers between devices: 33.5 us -> none  [the longest x4 19.6 us: extended_2(): after = lax.ppermute(leading, axis, down)]
    dot_general x15 -> x0, matrix products: 27.4 us -> none  [the longest x1 6.89 us: on_device(): jnp.dot(mix_grad, down_proj.T, preferred_element_type=jnp.float32)]
    add x2 -> x0, other arithmetic: 21.1 us -> none  [the longest x1 20.2 us: on_device(): back_sum + padded[9 - tap_row:12 - tap_row + row_count, 9 - tap_col:9 - t...]
  transfers between devices with their start and end apart: 11 -> 0, of which waited for: 4 -> 0; matrix products, arithmetic and copies ran while one was open for 11% -> 0% of each run, Pallas kernels for 0% -> 0%
where the time goes in v1:
time: 108 us; the launch traced here: 107 us
  Pallas kernels  96.7 us (90%)
  local copies, waits for them, and re-layouts  9.21 us (9%)
    pallas_call x1, Pallas kernels, on_device(): pl.pallas_call(functools.partial(kernel, factor), out_shape=(jax.ShapeDty...  96.7 us
    unnamed x17, local copies, waits for them, and re-layouts  5.9 us

profile of v1, /device:TPU:1, one launch (start us, length us, event | category | flops | bytes accessed | tf_op | source)
XLA Modules:
  0.0 107.3 jit_solution(13741624359212165319)
XLA Ops:
  0.6 0.0 copy-start.5
  0.6 0.7 copy-done.5
  1.3 0.6 reshape.32.bias_in
  1.9 0.0 copy-start.4
  1.9 0.7 convert_element_type.3
  2.6 0.0 copy-done.4
  2.6 0.6 copy.23
  3.2 0.1 copy.22
  3.3 0.7 reshape.30.land
  4.0 96.7 %shard_map.172 = (bf16[64,128]{1,0:T(8,128)(2,1)}, bf16[128,32,128]{2,1,0:T(8,128)(2,1)}, f32[49,128]{1,0:T(8,128)}, f32[128,512]{1,0:T(8,128)}, f32[512,128]{1,0:T(8,128)}, /*index=5*/f32[3,512,128]{2,1,0:T(8,128)}) custom-call(s32[2048]{0:T(1024)} %mirror.1, bf16[128,32,128]{2,1,0:T(8,128)(2,1)} %field.1, f32[16,256]{1,0:T(8,128)} %reshape.30.land, ...), custom_call_target="tpu_custom_call" | custom-call | tf_op jit(solution)/shard_map/pallas_call | solution.py:818
  100.7 1.3 %copy.26 = bf16[4,16,128]{2,0,1:T(4,128)(2,1)} copy(bf16[4,16,128]{2,1,0:T(8,128)(2,1)} %bitcast.11) | data formatting | bytes 32768 | tf_op jit(solution)/shard_map/reshape | solution.py:849
  102.0 0.0 copy-start.3
  102.0 0.0 copy-start.2
  102.0 0.0 copy-start.1
  102.0 2.3 %copy.32 = bf16[128,32,128]{2,1,0:T(8,128)(2,1)} copy(bf16[128,32,128]{2,1,0:T(8,128)(2,1)} %get-tuple-element.25) | data formatting | bytes 2097152
  104.4 0.0 copy-done.3
  104.4 0.0 copy-start
  104.4 0.6 copy.33
  105.0 0.0 copy-done.2
  105.0 0.7 copy.34
  105.7 0.0 copy-done.1
  105.7 0.7 copy.35
  106.4 0.0 copy-done
  106.4 0.9 copy.36
Async XLA Ops:
  0.6 0.7 copy-start.5
  1.9 0.7 copy-start.4
  102.0 2.3 %copy-start.3 = (f32[49,128]{1,0:T(8,128)S(1)}, f32[49,128]{1,0:T(8,128)}, u32[]{:S(2)}) copy-start(f32[49,128]{1,0:T(8,128)} %get-tuple-element.26) | copy-start | bytes 75268
  102.0 2.9 %copy-start.2 = (f32[128,512]{1,0:T(8,128)S(1)}, f32[128,512]{1,0:T(8,128)}, u32[]{:S(2)}) copy-start(f32[128,512]{1,0:T(8,128)} %get-tuple-element.27) | copy-start | bytes 786436
  102.0 3.6 %copy-start.1 = (f32[512,128]{1,0:T(8,128)S(1)}, f32[512,128]{1,0:T(8,128)}, u32[]{:S(2)}) copy-start(f32[512,128]{1,0:T(8,128)} %get-tuple-element.28) | copy-start | bytes 786436
  104.4 2.0 %copy-start = (f32[3,512,128]{2,1,0:T(8,128)S(1)}, f32[3,512,128]{2,1,0:T(8,128)}, u32[]{:S(2)}) copy-start(f32[3,512,128]{2,1,0:T(8,128)} %get-tuple-element.29) | copy-start | bytes 2359300

commit v2 on v1

--- a/solution.py
+++ b/solution.py
@@ -22,30 +22,38 @@
 ER = RR + 6
 NZ = 8
 NH = 8
-M = 256
+M = 512
 CHUNKS = RR * CC * G // M
 POS = M // G
 
 
-def norm_parts(values):
-    center = values - jnp.mean(values, axis=-1, keepdims=True)
-    rstd = lax.rsqrt(jnp.mean(center * center, axis=-1, keepdims=True) + epsilon)
+def mean_mx(values):
+    ones = jnp.full((C, C), 1.0 / C, BF16)
+    return dot(values.astype(BF16), ones, 1, 0)
+
+
+def norm_parts(values, exact=False):
+    mean = mean_mx(values) if exact else jnp.mean(values, axis=-1, keepdims=True)
+    center = values - mean
+    rstd = lax.rsqrt(mean_mx(center * center) + epsilon)
     return center * rstd, rstd
 
 
 def norm_back(grad_hat, normed_hat, rstd):
-    first = jnp.mean(grad_hat, axis=-1, keepdims=True)
-    second = jnp.mean(grad_hat * normed_hat, axis=-1, keepdims=True)
-    return rstd * (grad_hat - first - normed_hat * second)
+    return rstd * (grad_hat - mean_mx(grad_hat) - normed_hat * mean_mx(grad_hat * normed_hat))
 
 
 def gelu_parts(h):
-    e = jnp.exp(h * h * -0.5)
-    t = 1.0 / (1.0 + jnp.abs(h) * 0.23164189)
-    q = ((((0.5307027145 * t - 0.726576013) * t + 0.7107068705) * t - 0.142248368) * t + 0.127414796) * t
-    q = q * e
-    cdf = jnp.where(h >= 0.0, 1.0 - q, q)
-    return h * cdf, cdf + h * (e * 0.3989422804014327)
+    h = h.astype(BF16)
+    e = jnp.exp2(h * h * jnp.asarray(-0.7213475204444817, BF16))
+    cdf = jnp.asarray(0.5, BF16) + jnp.asarray(0.5, BF16) * lax.erf(h * jnp.asarray(0.7071067811865476, BF16))
+    return h * cdf, cdf + h * (e * jnp.asarray(0.3989422804014327, BF16))
+
+
+def tree(terms):
+    while len(terms) > 1:
+        terms = [a + b for a, b in zip(terms[::2], terms[1::2])] + terms[len(terms) & ~1 :]
+    return terms[0]
 
 
 def dot(a, b, ca, cb):
@@ -78,32 +86,18 @@
     gdown,
     gsec,
     fbuf,
-    ext,
-    ext2,
+    d32,
     obuf,
     sh,
-    wb,
     hat,
     rstd,
-    normed,
-    act,
-    slope,
     landb,
-    lev0,
-    lev1,
-    lev2,
     hat1,
     rstd1,
     hat2,
     rstd2,
     hat3,
     rstd3,
-    p1,
-    p2,
-    p3,
-    back1,
-    back2,
-    direct,
     dgb,
     upacc,
     dtacc,
@@ -156,6 +150,21 @@
     hr2,
     ssem,
     rsem,
+    ext,
+    ext2,
+    wb,
+    normed,
+    act,
+    slope,
+    lev0,
+    lev1,
+    lev2,
+    p1,
+    p2,
+    p3,
+    back1,
+    back2,
+    direct,
 ):
     lat = lax.axis_index("lat")
     lon = lax.axis_index("lon")
@@ -308,7 +317,7 @@
 
     tapf = taps_in[...].astype(F32)
     for t in range(49):
-        wb[t] = jnp.broadcast_to(tapf[t : t + 1], (G, C))
+        wb[t] = jnp.broadcast_to(tapf[t : t + 1], (G, C)).astype(BF16)
     gain = gain_in[...].astype(F32)
     bias = bias_in[...].astype(F32)
     scale = scale_in[...].astype(F32)
@@ -325,7 +334,7 @@
             for c in range(c0, c1):
                 ext[rows((r * EC + c) * G, G), :] = fbuf[
                     pl.ds(r * PITCH + 5 + c, G, stride=RR * PITCH), :
-                ]
+                ].astype(BF16)
 
     halo_wait(halo)
     for j in range(3):
@@ -358,11 +367,13 @@
     def conv(src, r, cb, flip):
         total_ = None
         for a in range(7):
+            terms = []
             for b in range(7):
                 t = 48 - (7 * a + b) if flip else 7 * a + b
                 x = src[rows(((r + a) * EC + cb * 8 + b) * G, 8 * G), :].reshape(8, G, C)
-                term = x * wb[t][None]
-                total_ = term if total_ is None else total_ + term
+                terms.append(x * wb[t][None])
+            term = tree(terms).astype(F32)
+            total_ = term if total_ is None else total_ + term
         return total_
 
     def depth_rows(r0, r1):
@@ -370,11 +381,7 @@
         def _(r):
             @pl.loop(0, 4)
             def _(cb):
-                h, s = norm_parts(conv(ext, r, cb, False).reshape(8 * G, C))
-                at = rows((r * CC + cb * 8) * G, 8 * G)
-                hat[at, :] = h
-                rstd[at, :] = jnp.broadcast_to(s, h.shape)
-                normed[at, :] = (h * gain).astype(BF16)
+                hat[rows((r * CC + cb * 8) * G, 8 * G), :] = conv(ext, r, cb, False).reshape(8 * G, C)
 
     depth_rows(0, 5)
 
@@ -391,14 +398,17 @@
     @pl.loop(0, CHUNKS)
     def _(k):
         at = rows(k * M, M)
-        r, c0 = k // 2, lax.rem(k, 2) * POS
-        h = dot(normed[at, :], up[...], 1, 0) + bias
-        active, slp = gelu_parts(h)
-        active = active.astype(BF16)
+        r = k
+        dh, ds = norm_parts(hat[at, :])
+        hat[at, :] = dh
+        rstd[at, :] = ds
+        nm = (dh * gain).astype(BF16)
+        normed[at, :] = nm
+        active, slp = gelu_parts(dot(nm, up[...], 1, 0) + bias)
         act[at, :] = active
-        slope[at, :] = slp.astype(BF16)
+        slope[at, :] = slp
         mixed = dot(active, down[...], 1, 0)
-        x = ext[rows(((r + 3) * EC + 3 + c0) * G, M), :]
+        x = ext[rows(((r + 3) * EC + 3) * G, M), :].astype(F32)
         lev0[at, :] = (landb[at, :] * (x + scale * mixed)).astype(BF16)
 
     def section(s, count, cols, src, hats, rstds, patches, put):
@@ -411,9 +421,9 @@
             parts = []
             for a in range(2):
                 at = rows((2 * i + a) * n, n)
-                h, rs_ = norm_parts(src[at, :].astype(F32))
+                h, rs_ = norm_parts(src[at, :].astype(F32), True)
                 hats[at, :] = h
-                rstds[at, :] = jnp.broadcast_to(rs_, h.shape)
+                rstds[at, :] = rs_
                 sn = (h * sg).astype(BF16).reshape(half, 2, G, C)
                 parts += [sn[:, b].reshape(half * G, C) for b in range(2)]
             p = jnp.concatenate(parts, axis=1)
@@ -442,12 +452,12 @@
         sg = sgain_in[s : s + 1].astype(F32)
         n = cols * G
         half = cols // 2
-        secacc[s] = jnp.zeros((4 * C, C), F32)
+        secacc[s] = jnp.zeros((C, 4 * C), F32)
 
         def step(i):
             at = rows(i * half * G, half * G)
             u = src[at, :]
-            secacc[s] += dot(patches[at, :], u, 0, 0)
+            secacc[s] += dot(u, patches[at, :], 0, 0)
             spread = dot(u, sw[s], 1, 1)
             for a in range(2):
                 at2 = rows((2 * i + a) * n, n)
@@ -456,8 +466,9 @@
                 outs = []
                 for b in range(2):
                     q = 2 * a + b
-                    g = (spread[:, q * C : (q + 1) * C] * sg).reshape(half, G, C)
-                    outs.append(norm_back(g, hh[:, b], rr[:, b]).astype(BF16))
+                    g = spread[:, q * C : (q + 1) * C] * sg
+                    back = norm_back(g, hh[:, b].reshape(half * G, C), rr[:, b].reshape(half * G, C))
+                    outs.append(back.astype(BF16).reshape(half, G, C))
                 put(at2, jnp.stack(outs, axis=1).reshape(n, C))
 
         if count == 1:
@@ -484,19 +495,20 @@
     @pl.loop(0, CHUNKS)
     def _(k):
         at = rows(k * M, M)
-        r, c0 = k // 2, lax.rem(k, 2) * POS
+        r = k
         mg = (direct[at, :].astype(F32) * scale).astype(BF16)
         dtacc[...] += dot(mg, act[at, :], 0, 0)
         hg = (dot(mg, down[...], 1, 1) * slope[at, :].astype(F32)).astype(BF16)
         upacc[...] += dot(normed[at, :], hg, 0, 0)
         ng = dot(hg, up[...], 1, 1) * gain
         dg = norm_back(ng, hat[at, :], rstd[at, :]).astype(BF16)
-        dgb[r, pl.ds(c0, POS)] = dg.reshape(POS, G, C)
-        ext2[rows(((r + 3) * EC + 3 + c0) * G, M), :] = dg.astype(F32)
+        dgb[r] = dg.reshape(POS, G, C)
+        ext2[rows(((r + 3) * EC + 3) * G, M), :] = dg
+        d32[rows((r * EC + 3) * G, M), :] = dg.astype(F32)
 
     for i in range(3):
-        rst[i] = ext2[pl.ds(((8 + i) * EC + 3) * G + 15, CC, stride=G), :].astype(BF16)
-        rsb[i] = ext2[pl.ds(((3 + i) * EC + 3) * G, CC, stride=G), :].astype(BF16)
+        rst[i] = d32[pl.ds(((5 + i) * EC + 3) * G + 15, CC, stride=G), :].astype(BF16)
+        rsb[i] = d32[pl.ds((i * EC + 3) * G, CC, stride=G), :].astype(BF16)
 
     halo2 = halo_copies(
         [
@@ -516,7 +528,8 @@
         a32[pl.ds(q * C, C), :] = upacc[:, q * C : (q + 1) * C]
         a32[pl.ds((4 + q) * C, C), :] = dtacc[:, q * C : (q + 1) * C].T
     for s in range(3):
-        a32[pl.ds((8 + 4 * s) * C, 4 * C), :] = secacc[s]
+        for q in range(4):
+            a32[pl.ds((8 + 4 * s + q) * C, C), :] = secacc[s, :, q * C : (q + 1) * C].T
     s1[...] = a32[...].astype(BF16)
 
     core_to, x_to = (lat + 1 - 2 * core, lon), (lax.rem(lat + 2, 4), lon)
@@ -528,11 +541,13 @@
         def _(r):
             @pl.loop(0, 4)
             def _(cb):
-                d = ext2[rows(((r + 3) * EC + 3 + cb * 8) * G, 8 * G), :]
+                d = ext2[rows(((r + 3) * EC + 3 + cb * 8) * G, 8 * G), :].reshape(8, G, C)
                 for a in range(7):
                     for b in range(7):
                         x = ext[rows(((r + a) * EC + cb * 8 + b) * G, 8 * G), :]
-                        tapacc[7 * a + b] += jnp.sum((x * d).reshape(16, 8, C), axis=0)
+                        p = x.reshape(8, G, C) * d
+                        t = tree([p[i] for i in range(8)]).astype(F32)
+                        tapacc[7 * a + b] += t[:8] + t[8:]
 
     tapacc[...] = jnp.zeros_like(tapacc)
     sum_taps(0, 2)
@@ -597,8 +612,10 @@
     @pl.loop(0, RR)
     def _(r):
         for j in range(3):
-            ext2[rows(((r + 3) * EC + j) * G, G), :] = dcl[r, j].astype(F32)
-            ext2[rows(((r + 3) * EC + 3 + CC + j) * G, G), :] = dcr[r, j].astype(F32)
+            ext2[rows(((r + 3) * EC + j) * G, G), :] = dcl[r, j]
+            ext2[rows(((r + 3) * EC + 3 + CC + j) * G, G), :] = dcr[r, j]
+            d32[rows((r * EC + j) * G, G), :] = dcl[r, j].astype(F32)
+            d32[rows((r * EC + 3 + CC + j) * G, G), :] = dcr[r, j].astype(F32)
 
     fg1, fg2, fg3 = fold_exchange(fg, hr1, hs2, hr2, CC)
 
@@ -606,12 +623,12 @@
     def _():
         for i in range(3):
             for cut, at in ((0, 0), (8, 8), (16, 16), (24, 24), (30, 30)):
-                zbuf[i, pl.ds(at, 8), :] = ext2[pl.ds(((8 + i) * EC + cut) * G + 15, 8, stride=G), :]
+                zbuf[i, pl.ds(at, 8), :] = d32[pl.ds(((5 + i) * EC + cut) * G + 15, 8, stride=G), :]
         for k in range(1, 4):
             total_ = None
             for a in range(k + 3, 7):
                 for b in range(7):
-                    term = zbuf[k - a + 5, pl.ds(6 - b, CC), :] * wb[7 * a + b][0:1]
+                    term = zbuf[k - a + 5, pl.ds(6 - b, CC), :] * tapf[7 * a + b : 7 * a + b + 1]
                     total_ = term if total_ is None else total_ + term
             fg[k - 1] = total_.astype(BF16)
         fg1()
@@ -623,7 +640,7 @@
         i = k if low else k - 3
         line = 7 if low else 24
         for c in range(EC):
-            sh[pl.ds(c * 32 + 8, G), :] = ext2[pl.ds(((r + 3) * EC + c) * G, G), :]
+            sh[pl.ds(c * 32 + 8, G), :] = d32[pl.ds((r * EC + c) * G, G), :]
         sh[pl.ds(3 * 32 + line, CC, stride=32), :] = edge[i].astype(F32)
         lft, rgt = el[i].astype(F32), er[i].astype(F32)
         for j in range(3):
@@ -631,7 +648,7 @@
             sh[pl.ds((CC + 3 + j) * 32 + line, 1), :] = rgt[j : j + 1]
         to = k if low else k + 8
         for c in range(EC):
-            ext2[pl.ds((to * EC + c) * G, G), :] = sh[pl.ds(c * 32 + (7 if low else 9), G), :]
+            ext2[pl.ds((to * EC + c) * G, G), :] = sh[pl.ds(c * 32 + (7 if low else 9), G), :].astype(BF16)
 
     def grad_rows(r0, r1_):
         @pl.loop(r0, r1_)
@@ -736,36 +753,22 @@
     sems = 96
     scratch = dict(
         fbuf=f(134 * PITCH, C),
-        ext=f(ER * EC * G, C),
-        ext2=f(ER * EC * G, C),
+        d32=f(RR * EC * G, C),
         obuf=f(n, C),
         sh=f(EC * 32, C),
-        wb=f(49, G, C),
         hat=f(n, C),
         rstd=f(n, C),
-        normed=h(n, C),
-        act=h(n, 512),
-        slope=h(n, 512),
         landb=f(n, C),
-        lev0=h(n, C),
-        lev1=h(n // 4, C),
-        lev2=h(n // 16, C),
         hat1=f(n, C),
         rstd1=f(n, C),
         hat2=f(n // 4, C),
         rstd2=f(n // 4, C),
         hat3=f(n // 16, C),
         rstd3=f(n // 16, C),
-        p1=h(n // 4, 512),
-        p2=h(n // 16, 512),
-        p3=h(n // 64, 512),
-        back1=h(n // 4, C),
-        back2=h(n // 16, C),
-        direct=h(n, C),
         dgb=h(RR, CC, G, C),
         upacc=f(C, 512),
         dtacc=f(C, 512),
-        secacc=f(3, 512, C),
+        secacc=f(3, C, 512),
         tapacc=f(49, 8, C),
         a32=f(2560, C),
         s1=h(2560, C),
@@ -815,8 +818,29 @@
         ssem=pltpu.SemaphoreType.DMA((sems,)),
         rsem=pltpu.SemaphoreType.DMA((sems,)),
     )
+    scoped = dict(
+        ext=h(ER * EC * G, C),
+        ext2=h(ER * EC * G, C),
+        wb=h(49, G, C),
+        normed=h(n, C),
+        act=h(n, 512),
+        slope=h(n, 512),
+        lev0=h(n, C),
+        lev1=h(n // 4, C),
+        lev2=h(n // 16, C),
+        p1=h(n // 4, 512),
+        p2=h(n // 16, 512),
+        p3=h(n // 64, 512),
+        back1=h(n // 4, C),
+        back2=h(n // 16, C),
+        direct=h(n, C),
+    )
+
+    def whole(*refs):
+        pl.run_scoped(functools.partial(kernel, factor, *refs), **scoped)
+
     bott, gfield, gtaps, gup, gdown, gsec = pl.pallas_call(
-        functools.partial(kernel, factor),
+        whole,
         out_shape=(
             jax.ShapeDtypeStruct((4 * G, C), BF16),
             jax.ShapeDtypeStruct((128, CC, C), BF16),

time: 108 us -> 94.8 us (0.88)
  the two profiles are of different devices: /device:TPU:1 before, /device:TPU:8 now
where the time goes in v2:
time: 94.8 us; the launch traced here: 94.4 us
  Pallas kernels  83.8 us (88%)
  local copies, waits for them, and re-layouts  9.21 us (10%)
    pallas_call x1, Pallas kernels, on_device(): pl.pallas_call(whole, out_shape=(jax.ShapeDtypeStruct((4 * G, C), BF16),...  83.8 us
    unnamed x17, local copies, waits for them, and re-layouts  5.9 us

profile of v2, /device:TPU:8, one launch (start us, length us, event | category | flops | bytes accessed | tf_op | source)
XLA Modules:
  0.0 94.4 jit_solution(10168445837326989609)
XLA Ops:
  0.6 0.0 copy-start.5
  0.6 0.7 copy-done.5
  1.3 0.6 reshape.32.refs_6_
  1.9 0.0 copy-start.4
  1.9 0.7 convert_element_type.3
  2.6 0.0 copy-done.4
  2.6 0.6 copy.23
  3.2 0.1 copy.22
  3.3 0.7 reshape.30.refs_2_
  4.0 83.8 %shard_map.172 = (bf16[64,128]{1,0:T(8,128)(2,1)}, bf16[128,32,128]{2,1,0:T(8,128)(2,1)}, f32[49,128]{1,0:T(8,128)}, f32[128,512]{1,0:T(8,128)}, f32[512,128]{1,0:T(8,128)}, /*index=5*/f32[3,512,128]{2,1,0:T(8,128)}) custom-call(s32[2048]{0:T(1024)} %refs_0_.1, bf16[128,32,128]{2,1,0:T(8,128)(2,1)} %refs_1_.1, f32[16,256]{1,0:T(8,128)} %reshape.30.refs_2_, ...), custom_call_target="tpu_custom_call" | custom-call | tf_op jit(solution)/shard_map/pallas_call | solution.py:842
  87.8 1.3 %copy.26 = bf16[4,16,128]{2,0,1:T(4,128)(2,1)} copy(bf16[4,16,128]{2,1,0:T(8,128)(2,1)} %bitcast.11) | data formatting | bytes 32768 | tf_op jit(solution)/shard_map/reshape | solution.py:873
  89.2 0.0 copy-start.3
  89.2 0.0 copy-start.2
  89.2 0.0 copy-start.1
  89.2 2.3 %copy.32 = bf16[128,32,128]{2,1,0:T(8,128)(2,1)} copy(bf16[128,32,128]{2,1,0:T(8,128)(2,1)} %get-tuple-element.25) | data formatting | bytes 2097152
  91.5 0.0 copy-done.3
  91.5 0.0 copy-start
  91.5 0.6 copy.33
  92.1 0.0 copy-done.2
  92.1 0.7 copy.34
  92.8 0.0 copy-done.1
  92.8 0.7 copy.35
  93.5 0.0 copy-done
  93.5 0.9 copy.36
Async XLA Ops:
  0.6 0.7 copy-start.5
  1.9 0.7 copy-start.4
  89.2 2.3 %copy-start.3 = (f32[49,128]{1,0:T(8,128)S(1)}, f32[49,128]{1,0:T(8,128)}, u32[]{:S(2)}) copy-start(f32[49,128]{1,0:T(8,128)} %get-tuple-element.26) | copy-start | bytes 75268
  89.2 2.9 %copy-start.2 = (f32[128,512]{1,0:T(8,128)S(1)}, f32[128,512]{1,0:T(8,128)}, u32[]{:S(2)}) copy-start(f32[128,512]{1,0:T(8,128)} %get-tuple-element.27) | copy-start | bytes 786436
  89.2 3.6 %copy-start.1 = (f32[512,128]{1,0:T(8,128)S(1)}, f32[512,128]{1,0:T(8,128)}, u32[]{:S(2)}) copy-start(f32[512,128]{1,0:T(8,128)} %get-tuple-element.28) | copy-start | bytes 786436
  91.5 2.0 %copy-start = (f32[3,512,128]{2,1,0:T(8,128)S(1)}, f32[3,512,128]{2,1,0:T(8,128)}, u32[]{:S(2)}) copy-start(f32[3,512,128]{2,1,0:T(8,128)} %get-tuple-element.29) | copy-start | bytes 2359300

commit v3 on v2

--- a/solution.py
+++ b/solution.py
@@ -67,6 +67,24 @@
 def kernel(
     factor,
     mirror,
+    x_field,
+    x_land,
+    x_taps_in,
+    x_gain_in,
+    x_up,
+    x_bias_in,
+    x_down,
+    x_scale_in,
+    x_sgain_in,
+    x_sw,
+    x_sbias_in,
+    x_cot,
+    bott,
+    gfield,
+    gtaps,
+    gup,
+    gdown,
+    gsec,
     field,
     land,
     taps_in,
@@ -79,12 +97,7 @@
     sw,
     sbias_in,
     cot,
-    bott,
-    gfield,
-    gtaps,
-    gup,
-    gdown,
-    gsec,
+    lsem,
     fbuf,
     d32,
     obuf,
@@ -103,19 +116,35 @@
     dtacc,
     secacc,
     tapacc,
-    a32,
-    s1,
-    r1,
-    s2f,
-    s2,
-    r2,
-    s3,
-    r3,
-    r4,
-    g3,
-    g2,
-    g1a,
-    g1b,
+    lt,
+    cb32,
+    cotb,
+    asec,
+    aden,
+    sec_s1,
+    sec_r1,
+    sec_s2f,
+    sec_s2,
+    sec_r2,
+    sec_s3,
+    sec_r3,
+    sec_r4,
+    sec_g3,
+    sec_g2,
+    sec_g1a,
+    sec_g1b,
+    den_s1,
+    den_r1,
+    den_s2f,
+    den_s2,
+    den_r2,
+    den_s3,
+    den_r3,
+    den_r4,
+    den_g3,
+    den_g2,
+    den_g1a,
+    den_g1b,
     tl,
     th,
     tz,
@@ -166,6 +195,28 @@
     back2,
     direct,
 ):
+    loads = [
+        pltpu.make_async_copy(a, b, lsem.at[i])
+        for i, (a, b) in enumerate(
+            (
+                (x_field, field),
+                (x_land, land),
+                (x_taps_in, taps_in),
+                (x_gain_in, gain_in),
+                (x_up, up),
+                (x_bias_in, bias_in),
+                (x_down, down),
+                (x_scale_in, scale_in),
+                (x_sgain_in, sgain_in),
+                (x_sw, sw),
+                (x_sbias_in, sbias_in),
+                (x_cot, cot),
+            )
+        )
+    ]
+    for copy in loads:
+        copy.start()
+
     lat = lax.axis_index("lat")
     lon = lax.axis_index("lon")
     hi, z = lon // NZ, lax.rem(lon, NZ)
@@ -217,6 +268,8 @@
         greet(hi_peer(j)[1])
     for j in range(1, NZ):
         greet(z_peer(j)[1])
+
+    loads[0].wait()
 
     @pl.loop(0, 128)
     def _(i):
@@ -315,18 +368,27 @@
     fold1, fold2, fold3 = fold_exchange(field.at[pl.ds(125, 3)], fr1, fs2, fr2, CC + 6)
     pl.when(north)(fold1)
 
+    for copy in loads[1:]:
+        copy.wait()
+
     tapf = taps_in[...].astype(F32)
     for t in range(49):
         wb[t] = jnp.broadcast_to(tapf[t : t + 1], (G, C)).astype(BF16)
     gain = gain_in[...].astype(F32)
-    bias = bias_in[...].astype(F32)
+    bias = bias_in[...].astype(F32).reshape(1, 512)
     scale = scale_in[...].astype(F32)
 
-    @pl.loop(0, CHUNKS)
-    def _(k):
-        turned = pltpu.roll(land[...], lax.rem(256 - k * POS, 256), 1)
-        for j in range(POS):
-            landb[rows((k * POS + j) * G, G), :] = jnp.broadcast_to(turned[:, j : j + 1], (G, C))
+    lt[...] = jnp.concatenate([land[...].astype(F32), jnp.zeros((C - CC, C), F32)], axis=0).T
+
+    @pl.loop(0, RR)
+    def _(r):
+        v = lt[pl.ds(r, G, stride=RR), :]
+        for c in range(CC):
+            landb[rows((r * CC + c) * G, G), :] = jnp.broadcast_to(v[:, c : c + 1], (G, C))
+
+    for g in range(G):
+        cb32[pl.ds(g, 4, stride=G), :] = cot[g].astype(F32)
+    cotb[...] = cb32[...].astype(BF16)
 
     def gather_rows(r0, r1, c0, c1):
         @pl.loop(r0, r1)
@@ -363,6 +425,16 @@
 
     gather_rows(0, 11, 0, EC)
     pl.when(north)(fold2)
+
+    def last_rows():
+        @pl.when(north)
+        def _():
+            off = fold3()
+            for k in range(3):
+                for i in range(EC):
+                    fbuf[pl.ds((131 + k) * PITCH + 5 + i, 1), :] = fcat[2 - k, pl.ds(off + EC - 1 - i, 1), :]
+
+        gather_rows(11, 14, 0, EC)
 
     def conv(src, r, cb, flip):
         total_ = None
@@ -376,24 +448,13 @@
             total_ = term if total_ is None else total_ + term
         return total_
 
-    def depth_rows(r0, r1):
-        @pl.loop(r0, r1)
-        def _(r):
-            @pl.loop(0, 4)
-            def _(cb):
-                hat[rows((r * CC + cb * 8) * G, 8 * G), :] = conv(ext, r, cb, False).reshape(8 * G, C)
-
-    depth_rows(0, 5)
-
-    @pl.when(north)
-    def _():
-        off = fold3()
-        for k in range(3):
-            for i in range(EC):
-                fbuf[pl.ds((131 + k) * PITCH + 5 + i, 1), :] = fcat[2 - k, pl.ds(off + EC - 1 - i, 1), :]
-
-    gather_rows(11, 14, 0, EC)
-    depth_rows(5, 8)
+    @pl.loop(0, RR)
+    def _(r):
+        pl.when(r == 5)(last_rows)
+
+        @pl.loop(0, 4)
+        def _(cb):
+            hat[rows((r * CC + cb * 8) * G, 8 * G), :] = conv(ext, r, cb, False).reshape(8 * G, C)
 
     @pl.loop(0, CHUNKS)
     def _(k):
@@ -442,7 +503,11 @@
         lev2[rows(i * 128, 128), :] = v
 
     def put3(i, v):
-        bott[...] = v
+        v = v.astype(F32)
+        for j in range(4):
+            cb32[pl.ds(j, G, stride=4), :] = v[j * G : (j + 1) * G]
+        for g in range(G):
+            bott[g] = cb32[pl.ds(g * 4, 4), :].astype(BF16)
 
     section(0, 4, 32, lev0, hat1, rstd1, p1, put1)
     section(1, 2, 16, lev1, hat2, rstd2, p2, put2)
@@ -485,9 +550,99 @@
     def putb0(at, v):
         direct[at, :] = (landb[at, :] * v.astype(F32)).astype(BF16)
 
-    section_back(2, 1, 8, cot, hat3, rstd3, p3, putb2)
+    section_back(2, 1, 8, cotb, hat3, rstd3, p3, putb2)
     section_back(1, 2, 16, back2, hat2, rstd2, p2, putb1)
     section_back(0, 4, 32, back1, hat1, rstd1, p1, putb0)
+
+    bsec = dict(s1=sec_s1, r1=sec_r1, s2f=sec_s2f, s2=sec_s2, r2=sec_r2, s3=sec_s3, r3=sec_r3, r4=sec_r4, g3=sec_g3, g2=sec_g2, g1a=sec_g1a, g1b=sec_g1b)
+    bden = dict(s1=den_s1, r1=den_r1, s2f=den_s2f, s2=den_s2, r2=den_r2, s3=den_s3, r3=den_r3, r4=den_r4, g3=den_g3, g2=den_g2, g1a=den_g1a, g1b=den_g1b)
+    core_to, x_to = (lat + 1 - 2 * core, lon), (lax.rem(lat + 2, 4), lon)
+    far_to = (lax.rem(lat + 3 - 2 * core, 4), lon)
+
+    def reduction(size, full, b):
+        half, quarter, piece = size // 2, size // 4, size // 32
+        c1 = remote(b["s1"].at[rows((1 - core) * half, half)], b["r1"], take(1), core_to)
+        c2 = remote(b["s2"].at[rows((1 - xl) * quarter, quarter)], b["r2"], take(1), x_to)
+        sem3, sem4, sem5 = take(NH - 1), take(NZ - 1), take(NH - 1)
+        x6 = remote(b["g3"], b["g2"], take(1), x_to)
+        x7 = remote(b["g3"], b["g1a"], take(1), core_to)
+        x8 = remote(b["g3"], b["g1b"], take(1), far_to)
+
+        def first():
+            b["s1"][...] = full[...].astype(BF16)
+            c1.start()
+
+        def second():
+            c1.wait()
+            b["s2f"][...] = full[rows(core * half, half), :] + b["r1"][...].astype(F32)
+            b["s2"][...] = b["s2f"][...].astype(BF16)
+            c2.start()
+
+        def third():
+            c2.wait()
+            b["s3"][...] = (b["s2f"][rows(xl * quarter, quarter), :] + b["r2"][...].astype(F32)).astype(BF16)
+            for j in range(1, NH):
+                h, to = hi_peer(j)
+                remote(b["s3"].at[rows(h * piece, piece)], b["r3"].at[hi], sem3 + j - 1, to).start()
+            b["r3"][hi] = b["s3"][rows(hi * piece, piece), :]
+
+        def total8(buf):
+            part = buf[0].astype(F32)
+            for i in range(1, 8):
+                part = part + buf[i].astype(F32)
+            return part.astype(BF16)
+
+        def fourth():
+            for j in range(1, NH):
+                h = lax.rem(hi + NH - j, NH)
+                copy = remote(b["s3"].at[pl.ds(0, piece)], b["r3"].at[h], sem3 + j - 1, hi_peer(j)[1])
+                copy.wait_send()
+                copy.wait_recv()
+            b["r4"][z] = total8(b["r3"])
+            for j in range(1, NZ):
+                remote(b["r4"].at[z], b["r4"].at[z], sem4 + j - 1, z_peer(j)[1]).start()
+
+        def fifth():
+            for j in range(1, NZ):
+                t = lax.rem(z + NZ - j, NZ)
+                copy = remote(b["r4"].at[z], b["r4"].at[t], sem4 + j - 1, z_peer(j)[1])
+                copy.wait_send()
+                copy.wait_recv()
+            b["g3"][hi] = total8(b["r4"])
+            for j in range(1, NH):
+                remote(b["g3"].at[hi], b["g3"].at[hi], sem5 + j - 1, hi_peer(j)[1]).start()
+
+        def sixth():
+            for j in range(1, NH):
+                h = lax.rem(hi + NH - j, NH)
+                copy = remote(b["g3"].at[hi], b["g3"].at[h], sem5 + j - 1, hi_peer(j)[1])
+                copy.wait_send()
+                copy.wait_recv()
+            x6.start()
+            x7.start()
+            x8.start()
+
+        def last(out):
+            def place(c_, x_, v):
+                out[rows((c_ * 2 + x_) * quarter, quarter), :] = v.reshape(quarter, C).astype(F32) * factor
+
+            place(core, xl, b["g3"][...])
+            x7.wait()
+            place(1 - core, xl, b["g1a"][...])
+            x6.wait()
+            place(core, 1 - xl, b["g2"][...])
+            x8.wait()
+            place(1 - core, 1 - xl, b["g1b"][...])
+
+        return first, second, third, fourth, fifth, sixth, last
+
+    rs1, rs2, rs3, rs4, rs5, rs6, rs7 = reduction(1536, asec, bsec)
+    rd1, rd2, rd3, rd4, rd5, rd6, rd7 = reduction(1024, aden, bden)
+
+    for s in range(3):
+        for q in range(4):
+            asec[pl.ds((4 * s + q) * C, C), :] = secacc[s, :, q * C : (q + 1) * C].T
+    rs1()
 
     upacc[...] = jnp.zeros_like(upacc)
     dtacc[...] = jnp.zeros_like(dtacc)
@@ -505,6 +660,8 @@
         dgb[r] = dg.reshape(POS, G, C)
         ext2[rows(((r + 3) * EC + 3) * G, M), :] = dg
         d32[rows((r * EC + 3) * G, M), :] = dg.astype(F32)
+        pl.when(k == 1)(rs2)
+        pl.when(k == 5)(rs3)
 
     for i in range(3):
         rst[i] = d32[pl.ds(((5 + i) * EC + 3) * G + 15, CC, stride=G), :].astype(BF16)
@@ -525,53 +682,35 @@
     halo_start(halo2)
 
     for q in range(4):
-        a32[pl.ds(q * C, C), :] = upacc[:, q * C : (q + 1) * C]
-        a32[pl.ds((4 + q) * C, C), :] = dtacc[:, q * C : (q + 1) * C].T
-    for s in range(3):
-        for q in range(4):
-            a32[pl.ds((8 + 4 * s + q) * C, C), :] = secacc[s, :, q * C : (q + 1) * C].T
-    s1[...] = a32[...].astype(BF16)
-
-    core_to, x_to = (lat + 1 - 2 * core, lon), (lax.rem(lat + 2, 4), lon)
-    c1 = remote(s1.at[rows((1 - core) * 1280, 1280)], r1, take(1), core_to)
-    c1.start()
-
-    def sum_taps(r0, r1_):
-        @pl.loop(r0, r1_)
-        def _(r):
-            @pl.loop(0, 4)
-            def _(cb):
-                d = ext2[rows(((r + 3) * EC + 3 + cb * 8) * G, 8 * G), :].reshape(8, G, C)
-                for a in range(7):
-                    for b in range(7):
-                        x = ext[rows(((r + a) * EC + cb * 8 + b) * G, 8 * G), :]
-                        p = x.reshape(8, G, C) * d
-                        t = tree([p[i] for i in range(8)]).astype(F32)
-                        tapacc[7 * a + b] += t[:8] + t[8:]
+        aden[pl.ds(q * C, C), :] = upacc[:, q * C : (q + 1) * C]
+        aden[pl.ds((4 + q) * C, C), :] = dtacc[:, q * C : (q + 1) * C].T
+    rd1()
 
     tapacc[...] = jnp.zeros_like(tapacc)
-    sum_taps(0, 2)
-
-    c1.wait()
-    s2f[...] = a32[rows(core * 1280, 1280), :] + r1[...].astype(F32)
-    s2[...] = s2f[...].astype(BF16)
-    c2 = remote(s2.at[rows((1 - xl) * 640, 640)], r2, take(1), x_to)
-    c2.start()
-    sum_taps(2, 4)
-    c2.wait()
-    s3[...] = (s2f[rows(xl * 640, 640), :] + r2[...].astype(F32)).astype(BF16)
-    sem3 = take(NH - 1)
-    for j in range(1, NH):
-        h, to = hi_peer(j)
-        remote(s3.at[rows(h * 80, 80)], r3.at[hi], sem3 + j - 1, to).start()
-    r3[hi] = s3[rows(hi * 80, 80), :]
-    sum_taps(4, 8)
+
+    @pl.loop(0, RR)
+    def _(r):
+        @pl.loop(0, 4)
+        def _(cb):
+            d = ext2[rows(((r + 3) * EC + 3 + cb * 8) * G, 8 * G), :].reshape(8, G, C)
+            for a in range(7):
+                for b in range(7):
+                    x = ext[rows(((r + a) * EC + cb * 8 + b) * G, 8 * G), :]
+                    p = x.reshape(8, G, C) * d
+                    t = tree([p[i] for i in range(8)]).astype(F32)
+                    tapacc[7 * a + b] += t[:8] + t[8:]
+
+        pl.when(r == 1)(rs4)
+        pl.when(r == 2)(rd2)
+        pl.when(r == 6)(rd3)
+
+    rs5()
 
     def tap_stage(buf, peers, me):
         sem = take(len(peers))
 
         def start(value):
-            buf[me] = value
+            buf[me] = value.astype(BF16)
             for i, (_, to) in enumerate(peers):
                 remote(buf.at[me], buf.at[me], sem + i, to).start()
 
@@ -580,9 +719,9 @@
                 copy = remote(buf.at[me], buf.at[frm], sem + i, to)
                 copy.wait_send()
                 copy.wait_recv()
-            out = buf[0]
+            out = buf[0].astype(F32)
             for i in range(1, buf.shape[0]):
-                out = out + buf[i]
+                out = out + buf[i].astype(F32)
             return out
 
         return start, finish
@@ -650,62 +789,35 @@
         for c in range(EC):
             ext2[pl.ds((to * EC + c) * G, G), :] = sh[pl.ds(c * 32 + (7 if low else 9), G), :].astype(BF16)
 
-    def grad_rows(r0, r1_):
-        @pl.loop(r0, r1_)
-        def _(r):
-            @pl.loop(0, 4)
-            def _(cb):
-                v = conv(ext2, r, cb, True)
-                v = v + direct[rows((r * CC + cb * 8) * G, 8 * G), :].astype(F32).reshape(8, G, C)
-                for j in range(8):
-                    obuf[pl.ds(r * CC + cb * 8 + j, G, stride=RR * CC), :] = v[j]
-
-    for j in range(1, NH):
-        h = lax.rem(hi + NH - j, NH)
-        copy = remote(s3.at[pl.ds(0, 80)], r3.at[h], sem3 + j - 1, hi_peer(j)[1])
-        copy.wait_send()
-        copy.wait_recv()
-    part = r3[0].astype(F32)
-    for i in range(1, NH):
-        part = part + r3[i].astype(F32)
-    r4[z] = part.astype(BF16)
-    sem4 = take(NZ - 1)
-    for j in range(1, NZ):
-        remote(r4.at[z], r4.at[z], sem4 + j - 1, z_peer(j)[1]).start()
-    grad_rows(0, 2)
-
-    th_start(tl_finish())
-    pl.when(north)(fg2)
-    for j in range(1, NZ):
-        t = lax.rem(z + NZ - j, NZ)
-        copy = remote(r4.at[z], r4.at[t], sem4 + j - 1, z_peer(j)[1])
-        copy.wait_send()
-        copy.wait_recv()
-    part = r4[0].astype(F32)
-    for i in range(1, NZ):
-        part = part + r4[i].astype(F32)
-    g3[hi] = part.astype(BF16)
-    sem5 = take(NH - 1)
-    for j in range(1, NH):
-        remote(g3.at[hi], g3.at[hi], sem5 + j - 1, hi_peer(j)[1]).start()
-    grad_rows(2, 4)
-
-    tz_start(th_finish())
-    for j in range(1, NH):
-        h = lax.rem(hi + NH - j, NH)
-        copy = remote(g3.at[hi], g3.at[h], sem5 + j - 1, hi_peer(j)[1])
-        copy.wait_send()
-        copy.wait_recv()
-    x6 = remote(g3, g2, take(1), x_to)
-    x7 = remote(g3, g1a, take(1), core_to)
-    x8 = remote(g2, g1b, take(1), core_to)
-    x6.start()
-    x7.start()
-    grad_rows(4, 6)
-    x6.wait_recv()
-    x8.start()
-    gtaps[...] = tz_finish()[:49] * factor
-    grad_rows(6, 8)
+    @pl.loop(0, RR)
+    def _(r):
+        @pl.loop(0, 4)
+        def _(cb):
+            v = conv(ext2, r, cb, True)
+            v = v + direct[rows((r * CC + cb * 8) * G, 8 * G), :].astype(F32).reshape(8, G, C)
+            for j in range(8):
+                obuf[pl.ds(r * CC + cb * 8 + j, G, stride=RR * CC), :] = v[j]
+
+        @pl.when(r == 0)
+        def _():
+            rs6()
+            rd4()
+
+        @pl.when(r == 1)
+        def _():
+            th_start(tl_finish())
+            pl.when(north)(fg2)
+
+        pl.when(r == 3)(rd5)
+
+        @pl.when(r == 5)
+        def _():
+            tz_start(th_finish())
+            rd6()
+
+        @pl.when(r == 6)
+        def _():
+            rs7(gsec)
 
     @pl.when(north)
     def _():
@@ -719,28 +831,15 @@
     def _(i):
         gfield[i] = obuf[rows(i * CC, CC), :].astype(BF16)
 
-    x6.wait_send()
-    x7.wait()
-    x8.wait()
-
-    def place(c_, x_, v):
-        a32[rows((c_ * 2 + x_) * 640, 640), :] = v.reshape(640, C).astype(F32) * factor
-
-    place(core, xl, g3[...])
-    place(core, 1 - xl, g2[...])
-    place(1 - core, xl, g1a[...])
-    place(1 - core, 1 - xl, g1b[...])
+    rd7(aden)
     for q in range(4):
-        gup[:, q * C : (q + 1) * C] = a32[pl.ds(q * C, C), :]
-        gdown[pl.ds(q * C, C), :] = a32[pl.ds((4 + q) * C, C), :]
-    for s in range(3):
-        gsec[s] = a32[pl.ds((8 + 4 * s) * C, 4 * C), :]
+        gup[:, q * C : (q + 1) * C] = aden[pl.ds(q * C, C), :]
+    gdown[...] = aden[pl.ds(4 * C, 4 * C), :]
+    gtaps[...] = tz_finish()[:49] * factor
 
 
 def on_device(field, land, mirror, depth_weight, norm_gain, up_weight, up_bias, down_proj, layer_scale, section_gain, section_weight, section_bias, cotangent):
     factor = 1.0 / math.sqrt(512 * 2048 / 64.0)
-    land_t = land.astype(F32).reshape(G, RR * CC)
-    cot_t = jnp.transpose(cotangent, (1, 0, 2)).reshape(4 * G, C)
     vm = pl.BlockSpec(memory_space=pltpu.VMEM)
     n = RR * CC * G
 
@@ -750,8 +849,21 @@
     def h(*shape):
         return pltpu.VMEM(shape, BF16)
 
-    sems = 96
+    sems = 128
     scratch = dict(
+        field=h(128, CC, C),
+        land=pltpu.VMEM((CC, 128), jnp.int32),
+        taps_in=h(49, C),
+        gain_in=h(1, C),
+        up=h(C, 512),
+        bias_in=h(512),
+        down=h(512, C),
+        scale_in=h(1, C),
+        sgain_in=h(3, C),
+        sw=h(3, 512, C),
+        sbias_in=h(3, C),
+        cot=h(G, 4, C),
+        lsem=pltpu.SemaphoreType.DMA((12,)),
         fbuf=f(134 * PITCH, C),
         d32=f(RR * EC * G, C),
         obuf=f(n, C),
@@ -770,22 +882,38 @@
         dtacc=f(C, 512),
         secacc=f(3, C, 512),
         tapacc=f(49, 8, C),
-        a32=f(2560, C),
-        s1=h(2560, C),
-        r1=h(1280, C),
-        s2f=f(1280, C),
-        s2=h(1280, C),
-        r2=h(640, C),
-        s3=h(640, C),
-        r3=h(NH, 80, C),
-        r4=h(NZ, 80, C),
-        g3=h(NH, 80, C),
-        g2=h(NH, 80, C),
-        g1a=h(NH, 80, C),
-        g1b=h(NH, 80, C),
-        tl=f(4, 64, C),
-        th=f(NH, 64, C),
-        tz=f(NZ, 64, C),
+        lt=f(C, C),
+        cb32=f(64, C),
+        cotb=h(64, C),
+        asec=f(1536, C),
+        aden=f(1024, C),
+        sec_s1=h(1536, C),
+        sec_r1=h(768, C),
+        sec_s2f=f(768, C),
+        sec_s2=h(768, C),
+        sec_r2=h(384, C),
+        sec_s3=h(384, C),
+        sec_r3=h(NH, 48, C),
+        sec_r4=h(NZ, 48, C),
+        sec_g3=h(NH, 48, C),
+        sec_g2=h(NH, 48, C),
+        sec_g1a=h(NH, 48, C),
+        sec_g1b=h(NH, 48, C),
+        den_s1=h(1024, C),
+        den_r1=h(512, C),
+        den_s2f=f(512, C),
+        den_s2=h(512, C),
+        den_r2=h(256, C),
+        den_s3=h(256, C),
+        den_r3=h(NH, 32, C),
+        den_r4=h(NZ, 32, C),
+        den_g3=h(NH, 32, C),
+        den_g2=h(NH, 32, C),
+        den_g1a=h(NH, 32, C),
+        den_g1b=h(NH, 32, C),
+        tl=h(4, 64, C),
+        th=h(NH, 64, C),
+        tz=h(NZ, 64, C),
         stl=h(3, 128, C),
         str_=h(3, 128, C),
         cl=h(3, 128, C),
@@ -842,36 +970,58 @@
     bott, gfield, gtaps, gup, gdown, gsec = pl.pallas_call(
         whole,
         out_shape=(
-            jax.ShapeDtypeStruct((4 * G, C), BF16),
+            jax.ShapeDtypeStruct((G, 4, C), BF16),
             jax.ShapeDtypeStruct((128, CC, C), BF16),
             jax.ShapeDtypeStruct((49, C), F32),
             jax.ShapeDtypeStruct((C, 512), F32),
             jax.ShapeDtypeStruct((512, C), F32),
-            jax.ShapeDtypeStruct((3, 512, C), F32),
+            jax.ShapeDtypeStruct((1536, C), F32),
         ),
-        in_specs=[pl.BlockSpec(memory_space=pltpu.SMEM)] + [vm] * 12,
+        in_specs=[pl.BlockSpec(memory_space=pltpu.SMEM)] + [pl.BlockSpec(memory_space=pltpu.HBM)] * 12,
         out_specs=(vm,) * 6,
         scratch_shapes=list(scratch.values()),
         compiler_params=pltpu.CompilerParams(
-            collective_id=0, has_side_effects=True, vmem_limit_bytes=67043328
+            collective_id=0, has_side_effects=True, vmem_limit_bytes=50 * 1024 * 1024
         ),
     )(
         mirror,
-        field,
-        land_t,
-        depth_weight,
-        norm_gain.reshape(1, C),
-        up_weight,
-        up_bias.reshape(1, 512),
-        down_proj,
-        layer_scale.reshape(1, C),
-        section_gain,
-        section_weight,
-        section_bias,
-        cot_t,
+        *(
+            pltpu.with_memory_space_constraint(v, pltpu.HBM)
+            for v in (
+                field,
+                land.T,
+                depth_weight,
+                norm_gain.reshape(1, C),
+                up_weight,
+                up_bias,
+                down_proj,
+                layer_scale.reshape(1, C),
+                section_gain,
+                section_weight,
+                section_bias,
+                cotangent,
+            )
+        ),
     )
-    bott = jnp.transpose(bott.reshape(4, G, C), (1, 0, 2))
-    return bott, gfield, gtaps, gup, gdown, gsec
+    results = (bott, gfield, gtaps, gup, gdown, gsec)
+    anywhere = pl.BlockSpec(memory_space=pl.ANY)
+
+    def write(*refs):
+        copies = [pltpu.make_async_copy(refs[i], refs[6 + i], refs[12].at[i]) for i in range(6)]
+        for copy in copies:
+            copy.start()
+        for copy in copies:
+            copy.wait()
+
+    bott, gfield, gtaps, gup, gdown, gsec = pl.pallas_call(
+        write,
+        out_shape=tuple(jax.ShapeDtypeStruct(x.shape, x.dtype) for x in results),
+        in_specs=[vm] * 6,
+        out_specs=(anywhere,) * 6,
+        scratch_shapes=[pltpu.SemaphoreType.DMA((6,))],
+        compiler_params=pltpu.CompilerParams(vmem_limit_bytes=16 * 1024 * 1024),
+    )(*results)
+    return bott, gfield, gtaps, gup, gdown, gsec.reshape(3, 512, C)
 
 
 def solution(mesh):

time: 94.8 us -> 81.9 us (0.86)
  the two profiles are of different devices: /device:TPU:8 before, /device:TPU:1 now
where the time goes in v3:
time: 81.9 us; the launch traced here: 81.7 us
  Pallas kernels  80.4 us (98%)
    pallas_call x1, Pallas kernels, on_device(): pl.pallas_call(whole, out_shape=(jax.ShapeDtypeStruct((G, 4, C), BF16), j...  78.9 us

profile of v3, /device:TPU:1, one launch (start us, length us, event | category | flops | bytes accessed | tf_op | source)
XLA Modules:
  0.0 81.7 jit_solution(7307688960823851819)
XLA Ops:
  0.6 0.0 copy-start
  0.6 0.7 copy-done
  1.3 78.9 %shard_map.172 = (bf16[16,4,128]{2,1,0:T(4,128)(2,1)S(1)}, bf16[128,32,128]{2,1,0:T(8,128)(2,1)S(1)}, f32[49,128]{1,0:T(8,128)S(1)}, f32[128,512]{1,0:T(8,128)S(...) custom-call(s32[2048]{0:T(1024)S(1)} %copy-done, bf16[128,32,128]{2,1,0:T(8,128)(2,1)} %refs_1_.1, ...), custom_call_target="tpu_custom_call" | custom-call | tf_op jit(solution)/shard_map/pallas_call | solution.py:970
  80.2 1.5 %shard_map.173 = (bf16[16,4,128]{2,1,0:T(4,128)(2,1)}, bf16[128,32,128]{2,1,0:T(8,128)(2,1)}, f32[49,128]{1,0:T(8,128)}, f32[128,512]{1,0:T(8,128)}, f32[512,128]{1,0:T(8,128)}, /*index=5*/f32[1536,128]{1,0:T(8,128)}) custom-call(bf16[16,4,128]{2,1,0:T(4,128)(2,1)S(1)} %get-tuple-element.18.refs_0_, bf16[128,32,128]{2,1,0:T(8,128)(2,1)S(1)} %get-tuple-element.19.refs_1_, ...), custom_call_target="tpu_custom_call" | custom-call | tf_op jit(solution)/shard_map/pallas_call | solution.py:1016
Async XLA Ops:
  0.6 0.7 copy-start

commit v4 on v3

--- a/solution.py
+++ b/solution.py
@@ -35,12 +35,23 @@
 def norm_parts(values, exact=False):
     mean = mean_mx(values) if exact else jnp.mean(values, axis=-1, keepdims=True)
     center = values - mean
-    rstd = lax.rsqrt(mean_mx(center * center) + epsilon)
+    rstd = lax.rsqrt(jnp.mean(center * center, axis=-1, keepdims=True) + epsilon)
     return center * rstd, rstd
 
 
 def norm_back(grad_hat, normed_hat, rstd):
-    return rstd * (grad_hat - mean_mx(grad_hat) - normed_hat * mean_mx(grad_hat * normed_hat))
+    second = jnp.mean(grad_hat * normed_hat, axis=-1, keepdims=True)
+    return rstd * (grad_hat - mean_mx(grad_hat) - normed_hat * second)
+
+
+def norm_back_wide(grad_hat, normed_hat, rstd):
+    pair = jnp.concatenate([grad_hat.astype(BF16), (grad_hat * normed_hat).astype(BF16)], axis=1)
+    ones, zeros = jnp.full((C, C), 1.0 / C, BF16), jnp.zeros((C, C), BF16)
+    both = jnp.concatenate(
+        [jnp.concatenate([ones, zeros], axis=1), jnp.concatenate([zeros, ones], axis=1)], axis=0
+    )
+    means = dot(pair, both, 1, 0)
+    return rstd * (grad_hat - means[:, :C] - normed_hat * means[:, C:])
 
 
 def gelu_parts(h):
@@ -437,16 +448,22 @@
         gather_rows(11, 14, 0, EC)
 
     def conv(src, r, cb, flip):
-        total_ = None
-        for a in range(7):
-            terms = []
-            for b in range(7):
-                t = 48 - (7 * a + b) if flip else 7 * a + b
-                x = src[rows(((r + a) * EC + cb * 8 + b) * G, 8 * G), :].reshape(8, G, C)
-                terms.append(x * wb[t][None])
-            term = tree(terms).astype(F32)
-            total_ = term if total_ is None else total_ + term
-        return total_
+        outs = []
+        for c in range(8):
+            total_ = None
+            for group in ((0, 1), (2, 3), (4, 5, 6)):
+                terms = []
+                for a in group:
+                    line = []
+                    for b in range(7):
+                        t = 48 - (7 * a + b) if flip else 7 * a + b
+                        x = src[rows(((r + a) * EC + cb * 8 + c + b) * G, G), :].reshape(1, G, C)
+                        line.append(x * wb[t][None])
+                    terms.append(tree(line))
+                term = tree(terms).astype(F32)
+                total_ = term if total_ is None else total_ + term
+            outs.append(total_)
+        return jnp.concatenate(outs, axis=0)
 
     @pl.loop(0, RR)
     def _(r):
@@ -456,21 +473,27 @@
         def _(cb):
             hat[rows((r * CC + cb * 8) * G, 8 * G), :] = conv(ext, r, cb, False).reshape(8 * G, C)
 
-    @pl.loop(0, CHUNKS)
-    def _(k):
+    def forward1(k):
         at = rows(k * M, M)
-        r = k
         dh, ds = norm_parts(hat[at, :])
         hat[at, :] = dh
-        rstd[at, :] = ds
+        rstd[at, :] = jnp.broadcast_to(ds, dh.shape)
         nm = (dh * gain).astype(BF16)
         normed[at, :] = nm
         active, slp = gelu_parts(dot(nm, up[...], 1, 0) + bias)
         act[at, :] = active
         slope[at, :] = slp
+        return active
+
+    def forward2(k, active):
+        at = rows(k * M, M)
         mixed = dot(active, down[...], 1, 0)
-        x = ext[rows(((r + 3) * EC + 3) * G, M), :].astype(F32)
+        x = ext[rows(((k + 3) * EC + 3) * G, M), :].astype(F32)
         lev0[at, :] = (landb[at, :] * (x + scale * mixed)).astype(BF16)
+
+    @pl.loop(0, CHUNKS)
+    def _(k):
+        forward2(k, forward1(k))
 
     def section(s, count, cols, src, hats, rstds, patches, put):
         sg = sgain_in[s : s + 1].astype(F32)
@@ -484,7 +507,7 @@
                 at = rows((2 * i + a) * n, n)
                 h, rs_ = norm_parts(src[at, :].astype(F32), True)
                 hats[at, :] = h
-                rstds[at, :] = rs_
+                rstds[at, :] = jnp.broadcast_to(rs_, h.shape)
                 sn = (h * sg).astype(BF16).reshape(half, 2, G, C)
                 parts += [sn[:, b].reshape(half * G, C) for b in range(2)]
             p = jnp.concatenate(parts, axis=1)
@@ -647,19 +670,24 @@
     upacc[...] = jnp.zeros_like(upacc)
     dtacc[...] = jnp.zeros_like(dtacc)
 
+    def backward1(k):
+        at = rows(k * M, M)
+        mg = (direct[at, :].astype(F32) * scale).astype(BF16)
+        dtacc[...] += dot(mg, act[at, :], 0, 0)
+        return (dot(mg, down[...], 1, 1) * slope[at, :].astype(F32)).astype(BF16)
+
+    def backward2(k, hg):
+        at = rows(k * M, M)
+        upacc[...] += dot(normed[at, :], hg, 0, 0)
+        ng = dot(hg, up[...], 1, 1) * gain
+        dg = norm_back_wide(ng, hat[at, :], rstd[at, :]).astype(BF16)
+        dgb[k] = dg.reshape(POS, G, C)
+        ext2[rows(((k + 3) * EC + 3) * G, M), :] = dg
+        d32[rows((k * EC + 3) * G, M), :] = dg.astype(F32)
+
     @pl.loop(0, CHUNKS)
     def _(k):
-        at = rows(k * M, M)
-        r = k
-        mg = (direct[at, :].astype(F32) * scale).astype(BF16)
-        dtacc[...] += dot(mg, act[at, :], 0, 0)
-        hg = (dot(mg, down[...], 1, 1) * slope[at, :].astype(F32)).astype(BF16)
-        upacc[...] += dot(normed[at, :], hg, 0, 0)
-        ng = dot(hg, up[...], 1, 1) * gain
-        dg = norm_back(ng, hat[at, :], rstd[at, :]).astype(BF16)
-        dgb[r] = dg.reshape(POS, G, C)
-        ext2[rows(((r + 3) * EC + 3) * G, M), :] = dg
-        d32[rows((r * EC + 3) * G, M), :] = dg.astype(F32)
+        backward2(k, backward1(k))
         pl.when(k == 1)(rs2)
         pl.when(k == 5)(rs3)
 

time: 81.9 us -> 81.1 us (level)
  no operation moved by 1% of the time
where the time goes in v4:
time: 81.1 us; the launch traced here: 81 us
  Pallas kernels  79.7 us (98%)
    pallas_call x1, Pallas kernels, on_device(): pl.pallas_call(whole, out_shape=(jax.ShapeDtypeStruct((G, 4, C), BF16), j...  78.2 us

profile of v4, /device:TPU:1, one launch (start us, length us, event | category | flops | bytes accessed | tf_op | source)
XLA Modules:
  0.0 81.0 jit_solution(11526787867939950448)
XLA Ops:
  0.6 0.0 copy-start
  0.6 0.7 copy-done
  1.3 78.2 %shard_map.172 = (bf16[16,4,128]{2,1,0:T(4,128)(2,1)S(1)}, bf16[128,32,128]{2,1,0:T(8,128)(2,1)S(1)}, f32[49,128]{1,0:T(8,128)S(1)}, f32[128,512]{1,0:T(8,128)S(...) custom-call(s32[2048]{0:T(1024)S(1)} %copy-done, bf16[128,32,128]{2,1,0:T(8,128)(2,1)} %refs_1_.1, ...), custom_call_target="tpu_custom_call" | custom-call | tf_op jit(solution)/shard_map/pallas_call | solution.py:998
  79.5 1.5 %shard_map.173 = (bf16[16,4,128]{2,1,0:T(4,128)(2,1)}, bf16[128,32,128]{2,1,0:T(8,128)(2,1)}, f32[49,128]{1,0:T(8,128)}, f32[128,512]{1,0:T(8,128)}, f32[512,128]{1,0:T(8,128)}, /*index=5*/f32[1536,128]{1,0:T(8,128)}) custom-call(bf16[16,4,128]{2,1,0:T(4,128)(2,1)S(1)} %get-tuple-element.18.refs_0_, bf16[128,32,128]{2,1,0:T(8,128)(2,1)S(1)} %get-tuple-element.19.refs_1_, ...), custom_call_target="tpu_custom_call" | custom-call | tf_op jit(solution)/shard_map/pallas_call | solution.py:1044
Async XLA Ops:
  0.6 0.7 copy-start

commit v5 on v4

--- a/solution.py
+++ b/solution.py
@@ -133,29 +133,19 @@
     asec,
     aden,
     sec_s1,
-    sec_r1,
-    sec_s2f,
-    sec_s2,
-    sec_r2,
+    sec_rq,
     sec_s3,
     sec_r3,
     sec_r4,
     sec_g3,
-    sec_g2,
-    sec_g1a,
-    sec_g1b,
+    sec_ga,
     den_s1,
-    den_r1,
-    den_s2f,
-    den_s2,
-    den_r2,
+    den_rq,
     den_s3,
     den_r3,
     den_r4,
     den_g3,
-    den_g2,
-    den_g1a,
-    den_g1b,
+    den_ga,
     tl,
     th,
     tz,
@@ -409,6 +399,7 @@
                     pl.ds(r * PITCH + 5 + c, G, stride=RR * PITCH), :
                 ].astype(BF16)
 
+    gather_rows(3, 11, 3, 3 + CC)
     halo_wait(halo)
     for j in range(3):
         fbuf[pl.ds(3 * PITCH + 5 + j, 128, stride=PITCH), :] = cl[j].astype(F32)
@@ -434,7 +425,9 @@
                 fbuf[pl.ds((131 + k) * PITCH + 5 + j, 1), :] = cnl[j].astype(F32)[k : k + 1]
                 fbuf[pl.ds((131 + k) * PITCH + 8 + CC + j, 1), :] = cnr[j].astype(F32)[k : k + 1]
 
-    gather_rows(0, 11, 0, EC)
+    gather_rows(0, 3, 0, EC)
+    gather_rows(3, 11, 0, 3)
+    gather_rows(3, 11, 3 + CC, EC)
     pl.when(north)(fold2)
 
     def last_rows():
@@ -577,33 +570,32 @@
     section_back(1, 2, 16, back2, hat2, rstd2, p2, putb1)
     section_back(0, 4, 32, back1, hat1, rstd1, p1, putb0)
 
-    bsec = dict(s1=sec_s1, r1=sec_r1, s2f=sec_s2f, s2=sec_s2, r2=sec_r2, s3=sec_s3, r3=sec_r3, r4=sec_r4, g3=sec_g3, g2=sec_g2, g1a=sec_g1a, g1b=sec_g1b)
-    bden = dict(s1=den_s1, r1=den_r1, s2f=den_s2f, s2=den_s2, r2=den_r2, s3=den_s3, r3=den_r3, r4=den_r4, g3=den_g3, g2=den_g2, g1a=den_g1a, g1b=den_g1b)
-    core_to, x_to = (lat + 1 - 2 * core, lon), (lax.rem(lat + 2, 4), lon)
-    far_to = (lax.rem(lat + 3 - 2 * core, 4), lon)
-
+    bsec = dict(s1=sec_s1, rq=sec_rq, s3=sec_s3, r3=sec_r3, r4=sec_r4, g3=sec_g3, ga=sec_ga)
+    bden = dict(s1=den_s1, rq=den_rq, s3=den_s3, r3=den_r3, r4=den_r4, g3=den_g3, ga=den_ga)
     def reduction(size, full, b):
-        half, quarter, piece = size // 2, size // 4, size // 32
-        c1 = remote(b["s1"].at[rows((1 - core) * half, half)], b["r1"], take(1), core_to)
-        c2 = remote(b["s2"].at[rows((1 - xl) * quarter, quarter)], b["r2"], take(1), x_to)
+        quarter, piece = size // 4, size // 32
+        sem1, sem6 = take(3), take(3)
         sem3, sem4, sem5 = take(NH - 1), take(NZ - 1), take(NH - 1)
-        x6 = remote(b["g3"], b["g2"], take(1), x_to)
-        x7 = remote(b["g3"], b["g1a"], take(1), core_to)
-        x8 = remote(b["g3"], b["g1b"], take(1), far_to)
+
+        def lat_peer(j):
+            to = lax.rem(lat + j, 4)
+            return to, (to, lon)
 
         def first():
             b["s1"][...] = full[...].astype(BF16)
-            c1.start()
-
-        def second():
-            c1.wait()
-            b["s2f"][...] = full[rows(core * half, half), :] + b["r1"][...].astype(F32)
-            b["s2"][...] = b["s2f"][...].astype(BF16)
-            c2.start()
+            for j in range(1, 4):
+                t, to = lat_peer(j)
+                remote(b["s1"].at[rows(t * quarter, quarter)], b["rq"].at[lat], sem1 + j - 1, to).start()
 
         def third():
-            c2.wait()
-            b["s3"][...] = (b["s2f"][rows(xl * quarter, quarter), :] + b["r2"][...].astype(F32)).astype(BF16)
+            total_ = full[rows(lat * quarter, quarter), :]
+            for j in range(1, 4):
+                frm = lax.rem(lat + 4 - j, 4)
+                copy = remote(b["s1"].at[pl.ds(0, quarter)], b["rq"].at[frm], sem1 + j - 1, lat_peer(j)[1])
+                copy.wait_send()
+                copy.wait_recv()
+                total_ = total_ + b["rq"][frm].astype(F32)
+            b["s3"][...] = total_.astype(BF16)
             for j in range(1, NH):
                 h, to = hi_peer(j)
                 remote(b["s3"].at[rows(h * piece, piece)], b["r3"].at[hi], sem3 + j - 1, to).start()
@@ -641,26 +633,25 @@
                 copy = remote(b["g3"].at[hi], b["g3"].at[h], sem5 + j - 1, hi_peer(j)[1])
                 copy.wait_send()
                 copy.wait_recv()
-            x6.start()
-            x7.start()
-            x8.start()
+            for j in range(1, 4):
+                remote(b["g3"], b["ga"].at[lat], sem6 + j - 1, lat_peer(j)[1]).start()
 
         def last(out):
-            def place(c_, x_, v):
-                out[rows((c_ * 2 + x_) * quarter, quarter), :] = v.reshape(quarter, C).astype(F32) * factor
-
-            place(core, xl, b["g3"][...])
-            x7.wait()
-            place(1 - core, xl, b["g1a"][...])
-            x6.wait()
-            place(core, 1 - xl, b["g2"][...])
-            x8.wait()
-            place(1 - core, 1 - xl, b["g1b"][...])
-
-        return first, second, third, fourth, fifth, sixth, last
-
-    rs1, rs2, rs3, rs4, rs5, rs6, rs7 = reduction(1536, asec, bsec)
-    rd1, rd2, rd3, rd4, rd5, rd6, rd7 = reduction(1024, aden, bden)
+            def place(t, v):
+                out[rows(t * quarter, quarter), :] = v.reshape(quarter, C).astype(F32) * factor
+
+            place(lat, b["g3"][...])
+            for j in range(1, 4):
+                frm = lax.rem(lat + 4 - j, 4)
+                copy = remote(b["g3"], b["ga"].at[frm], sem6 + j - 1, lat_peer(j)[1])
+                copy.wait_send()
+                copy.wait_recv()
+                place(frm, b["ga"][frm])
+
+        return first, third, fourth, fifth, sixth, last
+
+    rs1, rs3, rs4, rs5, rs6, rs7 = reduction(1536, asec, bsec)
+    rd1, rd3, rd4, rd5, rd6, rd7 = reduction(1024, aden, bden)
 
     for s in range(3):
         for q in range(4):
@@ -688,8 +679,7 @@
     @pl.loop(0, CHUNKS)
     def _(k):
         backward2(k, backward1(k))
-        pl.when(k == 1)(rs2)
-        pl.when(k == 5)(rs3)
+        pl.when(k == 4)(rs3)
 
     for i in range(3):
         rst[i] = d32[pl.ds(((5 + i) * EC + 3) * G + 15, CC, stride=G), :].astype(BF16)
@@ -729,10 +719,8 @@
                     tapacc[7 * a + b] += t[:8] + t[8:]
 
         pl.when(r == 1)(rs4)
-        pl.when(r == 2)(rd2)
-        pl.when(r == 6)(rd3)
-
-    rs5()
+        pl.when(r == 4)(rd3)
+        pl.when(r == 6)(rs5)
 
     def tap_stage(buf, peers, me):
         sem = take(len(peers))
@@ -817,6 +805,8 @@
         for c in range(EC):
             ext2[pl.ds((to * EC + c) * G, G), :] = sh[pl.ds(c * 32 + (7 if low else 9), G), :].astype(BF16)
 
+    rd4()
+
     @pl.loop(0, RR)
     def _(r):
         @pl.loop(0, 4)
@@ -826,26 +816,20 @@
             for j in range(8):
                 obuf[pl.ds(r * CC + cb * 8 + j, G, stride=RR * CC), :] = v[j]
 
-        @pl.when(r == 0)
-        def _():
-            rs6()
-            rd4()
-
         @pl.when(r == 1)
         def _():
             th_start(tl_finish())
             pl.when(north)(fg2)
+            rs6()
 
         pl.when(r == 3)(rd5)
 
         @pl.when(r == 5)
         def _():
             tz_start(th_finish())
-            rd6()
-
-        @pl.when(r == 6)
-        def _():
             rs7(gsec)
+
+        pl.when(r == 6)(rd6)
 
     @pl.when(north)
     def _():
@@ -916,29 +900,19 @@
         asec=f(1536, C),
         aden=f(1024, C),
         sec_s1=h(1536, C),
-        sec_r1=h(768, C),
-        sec_s2f=f(768, C),
-        sec_s2=h(768, C),
-        sec_r2=h(384, C),
+        sec_rq=h(4, 384, C),
         sec_s3=h(384, C),
         sec_r3=h(NH, 48, C),
         sec_r4=h(NZ, 48, C),
         sec_g3=h(NH, 48, C),
-        sec_g2=h(NH, 48, C),
-        sec_g1a=h(NH, 48, C),
-        sec_g1b=h(NH, 48, C),
+        sec_ga=h(4, NH, 48, C),
         den_s1=h(1024, C),
-        den_r1=h(512, C),
-        den_s2f=f(512, C),
-        den_s2=h(512, C),
-        den_r2=h(256, C),
+        den_rq=h(4, 256, C),
         den_s3=h(256, C),
         den_r3=h(NH, 32, C),
         den_r4=h(NZ, 32, C),
         den_g3=h(NH, 32, C),
-        den_g2=h(NH, 32, C),
-        den_g1a=h(NH, 32, C),
-        den_g1b=h(NH, 32, C),
+        den_ga=h(4, NH, 32, C),
         tl=h(4, 64, C),
         th=h(NH, 64, C),
         tz=h(NZ, 64, C),

time: 81.1 us -> 77 us (0.949)
  Pallas kernels: 79.7 us -> 75.5 us
    pallas_call x1, Pallas kernels: 78.2 us -> 74 us  [on_device(): pl.pallas_call(whole, out_shape=(jax.ShapeDtypeStruct((G, 4, C), BF16), j...]
where the time goes in v5:
time: 77 us; the launch traced here: 76.8 us
  Pallas kernels  75.5 us (98%)
    pallas_call x1, Pallas kernels, on_device(): pl.pallas_call(whole, out_shape=(jax.ShapeDtypeStruct((G, 4, C), BF16), j...  74 us

profile of v5, /device:TPU:1, one launch (start us, length us, event | category | flops | bytes accessed | tf_op | source)
XLA Modules:
  0.0 76.8 jit_solution(18124434476894723018)
XLA Ops:
  0.6 0.0 copy-start
  0.6 0.7 copy-done
  1.3 74.0 %shard_map.172 = (bf16[16,4,128]{2,1,0:T(4,128)(2,1)S(1)}, bf16[128,32,128]{2,1,0:T(8,128)(2,1)S(1)}, f32[49,128]{1,0:T(8,128)S(1)}, f32[128,512]{1,0:T(8,128)S(...) custom-call(s32[2048]{0:T(1024)S(1)} %copy-done, bf16[128,32,128]{2,1,0:T(8,128)(2,1)} %refs_1_.1, ...), custom_call_target="tpu_custom_call" | custom-call | tf_op jit(solution)/shard_map/pallas_call | solution.py:972
  75.3 1.5 %shard_map.173 = (bf16[16,4,128]{2,1,0:T(4,128)(2,1)}, bf16[128,32,128]{2,1,0:T(8,128)(2,1)}, f32[49,128]{1,0:T(8,128)}, f32[128,512]{1,0:T(8,128)}, f32[512,128]{1,0:T(8,128)}, /*index=5*/f32[1536,128]{1,0:T(8,128)}) custom-call(bf16[16,4,128]{2,1,0:T(4,128)(2,1)S(1)} %get-tuple-element.18.refs_0_, bf16[128,32,128]{2,1,0:T(8,128)(2,1)S(1)} %get-tuple-element.19.refs_1_, ...), custom_call_target="tpu_custom_call" | custom-call | tf_op jit(solution)/shard_map/pallas_call | solution.py:1018
Async XLA Ops:
  0.6 0.7 copy-start

commit v6 on v5

--- a/solution.py
+++ b/solution.py
@@ -22,7 +22,7 @@
 ER = RR + 6
 NZ = 8
 NH = 8
-M = 512
+M = 1024
 CHUNKS = RR * CC * G // M
 POS = M // G
 
@@ -481,7 +481,7 @@
     def forward2(k, active):
         at = rows(k * M, M)
         mixed = dot(active, down[...], 1, 0)
-        x = ext[rows(((k + 3) * EC + 3) * G, M), :].astype(F32)
+        x = jnp.concatenate([ext[rows(((2 * k + 3 + i) * EC + 3) * G, M // 2), :].astype(F32) for i in range(2)], axis=0)
         lev0[at, :] = (landb[at, :] * (x + scale * mixed)).astype(BF16)
 
     @pl.loop(0, CHUNKS)
@@ -672,14 +672,16 @@
         upacc[...] += dot(normed[at, :], hg, 0, 0)
         ng = dot(hg, up[...], 1, 1) * gain
         dg = norm_back_wide(ng, hat[at, :], rstd[at, :]).astype(BF16)
-        dgb[k] = dg.reshape(POS, G, C)
-        ext2[rows(((k + 3) * EC + 3) * G, M), :] = dg
-        d32[rows((k * EC + 3) * G, M), :] = dg.astype(F32)
+        for i in range(2):
+            part = dg[i * M // 2 : (i + 1) * M // 2]
+            dgb[2 * k + i] = part.reshape(POS // 2, G, C)
+            ext2[rows(((2 * k + i + 3) * EC + 3) * G, M // 2), :] = part
+            d32[rows(((2 * k + i) * EC + 3) * G, M // 2), :] = part.astype(F32)
 
     @pl.loop(0, CHUNKS)
     def _(k):
         backward2(k, backward1(k))
-        pl.when(k == 4)(rs3)
+        pl.when(k == 2)(rs3)
 
     for i in range(3):
         rst[i] = d32[pl.ds(((5 + i) * EC + 3) * G + 15, CC, stride=G), :].astype(BF16)

time: 77 us -> 75.4 us (0.979)
  Pallas kernels: 75.5 us -> 73.9 us
    pallas_call x1, Pallas kernels: 74 us -> 72.4 us  [on_device(): pl.pallas_call(whole, out_shape=(jax.ShapeDtypeStruct((G, 4, C), BF16), j...]
where the time goes in v6:
time: 75.4 us; the launch traced here: 75.2 us
  Pallas kernels  73.9 us (98%)
    pallas_call x1, Pallas kernels, on_device(): pl.pallas_call(whole, out_shape=(jax.ShapeDtypeStruct((G, 4, C), BF16), j...  72.4 us

profile of v6, /device:TPU:1, one launch (start us, length us, event | category | flops | bytes accessed | tf_op | source)
XLA Modules:
  0.0 75.2 jit_solution(11004403545394625124)
XLA Ops:
  0.6 0.0 copy-start
  0.6 0.7 copy-done
  1.3 72.4 %shard_map.172 = (bf16[16,4,128]{2,1,0:T(4,128)(2,1)S(1)}, bf16[128,32,128]{2,1,0:T(8,128)(2,1)S(1)}, f32[49,128]{1,0:T(8,128)S(1)}, f32[128,512]{1,0:T(8,128)S(...) custom-call(s32[2048]{0:T(1024)S(1)} %copy-done, bf16[128,32,128]{2,1,0:T(8,128)(2,1)} %refs_1_.1, ...), custom_call_target="tpu_custom_call" | custom-call | tf_op jit(solution)/shard_map/pallas_call | solution.py:974
  73.7 1.5 %shard_map.173 = (bf16[16,4,128]{2,1,0:T(4,128)(2,1)}, bf16[128,32,128]{2,1,0:T(8,128)(2,1)}, f32[49,128]{1,0:T(8,128)}, f32[128,512]{1,0:T(8,128)}, f32[512,128]{1,0:T(8,128)}, /*index=5*/f32[1536,128]{1,0:T(8,128)}) custom-call(bf16[16,4,128]{2,1,0:T(4,128)(2,1)S(1)} %get-tuple-element.18.refs_0_, bf16[128,32,128]{2,1,0:T(8,128)(2,1)S(1)} %get-tuple-element.19.refs_1_, ...), custom_call_target="tpu_custom_call" | custom-call | tf_op jit(solution)/shard_map/pallas_call | solution.py:1020
Async XLA Ops:
  0.6 0.7 copy-start

commit v7 on v6

--- a/solution.py
+++ b/solution.py
@@ -721,8 +721,10 @@
                     tapacc[7 * a + b] += t[:8] + t[8:]
 
         pl.when(r == 1)(rs4)
-        pl.when(r == 4)(rd3)
+        pl.when(r == 3)(rd3)
         pl.when(r == 6)(rs5)
+
+    rd4()
 
     def tap_stage(buf, peers, me):
         sem = take(len(peers))
@@ -807,8 +809,6 @@
         for c in range(EC):
             ext2[pl.ds((to * EC + c) * G, G), :] = sh[pl.ds(c * 32 + (7 if low else 9), G), :].astype(BF16)
 
-    rd4()
-
     @pl.loop(0, RR)
     def _(r):
         @pl.loop(0, 4)
@@ -824,14 +824,16 @@
             pl.when(north)(fg2)
             rs6()
 
-        pl.when(r == 3)(rd5)
+        pl.when(r == 1)(rd5)
 
         @pl.when(r == 5)
         def _():
+            rs7(gsec)
+
+        @pl.when(r == 4)
+        def _():
+            rd6()
             tz_start(th_finish())
-            rs7(gsec)
-
-        pl.when(r == 6)(rd6)
 
     @pl.when(north)
     def _():

time: 75.4 us -> 76.5 us (1.015)
  Pallas kernels: 73.9 us -> 75 us
    pallas_call x1, Pallas kernels: 72.4 us -> 73.5 us  [on_device(): pl.pallas_call(whole, out_shape=(jax.ShapeDtypeStruct((G, 4, C), BF16), j...]
where the time goes in v7:
time: 76.5 us; the launch traced here: 76.3 us
  Pallas kernels  75 us (98%)
    pallas_call x1, Pallas kernels, on_device(): pl.pallas_call(whole, out_shape=(jax.ShapeDtypeStruct((G, 4, C), BF16), j...  73.5 us

profile of v7, /device:TPU:1, one launch (start us, length us, event | category | flops | bytes accessed | tf_op | source)
XLA Modules:
  0.0 76.3 jit_solution(15619347096378545874)
XLA Ops:
  0.6 0.0 copy-start
  0.6 0.7 copy-done
  1.3 73.5 %shard_map.172 = (bf16[16,4,128]{2,1,0:T(4,128)(2,1)S(1)}, bf16[128,32,128]{2,1,0:T(8,128)(2,1)S(1)}, f32[49,128]{1,0:T(8,128)S(1)}, f32[128,512]{1,0:T(8,128)S(...) custom-call(s32[2048]{0:T(1024)S(1)} %copy-done, bf16[128,32,128]{2,1,0:T(8,128)(2,1)} %refs_1_.1, ...), custom_call_target="tpu_custom_call" | custom-call | tf_op jit(solution)/shard_map/pallas_call | solution.py:976
  74.8 1.5 %shard_map.173 = (bf16[16,4,128]{2,1,0:T(4,128)(2,1)}, bf16[128,32,128]{2,1,0:T(8,128)(2,1)}, f32[49,128]{1,0:T(8,128)}, f32[128,512]{1,0:T(8,128)}, f32[512,128]{1,0:T(8,128)}, /*index=5*/f32[1536,128]{1,0:T(8,128)}) custom-call(bf16[16,4,128]{2,1,0:T(4,128)(2,1)S(1)} %get-tuple-element.18.refs_0_, bf16[128,32,128]{2,1,0:T(8,128)(2,1)S(1)} %get-tuple-element.19.refs_1_, ...), custom_call_target="tpu_custom_call" | custom-call | tf_op jit(solution)/shard_map/pallas_call | solution.py:1022
Async XLA Ops:
  0.6 0.7 copy-start
